TPU v7x, 32 devices: a whole 2x2x4 slice. The times are simulated.
32 devices in a mesh: ens: 2 (over x), lat: 4 (over z), lon: 4 (over y, core).
Axes of the slice: x: 2, y: 2, z: 4, core: 2. Of those that a mesh axis runs over, the one named last changes fastest.
Arguments:
- prior_states: bfloat16 [16, 40, 128, 1024], P('ens', None, 'lat', 'lon'), may hold values from -6 to 6
- measured_brightness: float32 [16, 64, 512], P(None, 'lat', 'lon'), may hold values from -16 to 16
- measured_indicator: int32 [64, 512], P('lat', 'lon'), may hold values 0 or 1
- sensor_error_spread: float32 [16], replicated, may hold values from 2 to 8
- entry_layer_stencil: bfloat16 [64, 40, 5, 5], replicated, may hold values from -0.25 to 0.25
- entry_layer_offset: float32 [64], replicated, may hold values from -3 to 3
- middle_layer_stencil: bfloat16 [64, 64, 3, 3], replicated, may hold values from -0.375 to 0.375
- middle_layer_offset: float32 [64], replicated, may hold values from -3 to 3
- brightness_matrix: bfloat16 [16, 64], replicated, may hold values from -0.75 to 0.75
- brightness_offset: float32 [16], replicated, may hold values from -3 to 3
- ancestor_indices: int32 [16, 4, 8], P(None, 'lat', 'lon'), may hold values from 0 to 15, as said below
Outputs:
- analysis: float32 [16, 40, 128, 1024], P('ens', None, 'lat', 'lon')
- weights: float32 [16, 64, 512], P('ens', 'lat', 'lon')
Inputs may be any that keep to these rules, and one draw needn't show every extreme that they name: `ancestor_indices`: in every localization tile, the 8 slots s with the same s // 8 take at most 4 parents from any one group of particles with the same p // 8, and exactly 4 from some group.
All inputs are finite; a program needn't handle non-finite values. No bound on the sum of `measured_indicator` on one device may be relied on, other than what follows from the above.
Results may differ from a plain program's by a relative error of at most 0.0085.
Values may be sent and summed in bfloat16 or wider, within the bound.
No kernel may reach another device: no remote copies, remote signals or barrier semaphores. Data moves between devices by JAX's collectives and lax.ppermute only.
A program may use at most 128 MiB of HBM per device.

v0:
```python
import jax
import jax.numpy as jnp
from jax import lax
from jax.experimental import pallas as pl
from jax.experimental.pallas import tpu as pltpu
from jax.sharding import PartitionSpec as P
import numpy as np

PATCH_NORTHWARD = 32
PATCH_EASTWARD = 128
RADIUS = 16


relax_factor = 0.6
PIECES = 4


def extended(shard, sides, width):
    for axis, dim in sides:
        peers, length = (lax.axis_size(axis), shard.shape[dim])
        up = [(i, (i + 1) % peers) for i in range(peers - 1)]
        down = [(j, i) for i, j in up]
        last = lax.slice_in_dim(shard, length - width, length, axis=dim)
        first = lax.slice_in_dim(shard, 0, width, axis=dim)
        before = lax.ppermute(last, axis, up)
        after = lax.ppermute(first, axis, down)
        shard = jnp.concatenate([before, shard, after], axis=dim)
    return shard


def taper_band(inner_count, radius):
    tap_count = 2 * radius + 1
    tap_width = radius / 2.0
    taps = np.exp(-0.5 * ((np.arange(tap_count) - radius) / tap_width) ** 2)
    taps = taps / taps.sum()
    band = np.zeros((inner_count, inner_count + 2 * radius), np.float32)
    for out_index in range(inner_count):
        band[out_index, out_index : out_index + tap_count] = taps
    return band


def expand_patches(values):
    lead = values.shape[:-2]
    rows, cols = (values.shape[-2], values.shape[-1])
    grown = jnp.broadcast_to(values[..., :, None, :, None], lead + (rows, 2, cols, 2))
    return grown.reshape(lead + (rows * 2, cols * 2))


LANES = 128


def store_doubled(out, values):
    count, rows, cols = values.shape
    of_cols = lax.broadcasted_iota(jnp.int32, (cols, 2 * cols), 0)
    to_cols = lax.broadcasted_iota(jnp.int32, (cols, 2 * cols), 1)
    wide = (lax.shift_right_logical(to_cols, 1) == of_cols).astype(jnp.float32)
    wide = wide.astype(jnp.bfloat16)
    rest = values.reshape(count * rows, cols)
    grown = None
    for _ in range(3):
        part = rest.astype(jnp.bfloat16)
        rest = rest - part.astype(jnp.float32)
        moved = jnp.dot(part, wide, preferred_element_type=jnp.float32)
        grown = moved if grown is None else grown + moved
    for which in range(count):
        for block in range(2 * cols // LANES):
            piece = grown[which * rows : (which + 1) * rows, block * LANES : (block + 1) * LANES]
            for half in range(2):
                out[which, block, pl.ds(half, rows, stride=2), :] = piece


def tiles_of(rows, cols):
    return [
        (north, east)
        for north in range(rows // PATCH_NORTHWARD)
        for east in range(cols // PATCH_EASTWARD)
    ]


def tile_window(north, east):
    return (
        pl.ds(north * PATCH_NORTHWARD, PATCH_NORTHWARD),
        pl.ds(east * PATCH_EASTWARD, PATCH_EASTWARD),
    )


def group_mean(borders, smooth, from_west, from_east, band, prior_states, pieces, chunk):
    members, pixel_rows, pixel_cols = smooth.shape
    _, heights, rows, cols = prior_states.shape
    blocks = cols // LANES
    per_piece = heights // chunk // pieces

    def kernel(border, own_ref, left, right, band_ref, prior, scaled_ref, norm_ref, mean_ref, *refs):
        sent, share = refs[:pieces], refs[pieces]
        step = pl.program_id(0)

        @pl.when(step == 0)
        def _():
            west = jnp.where(border[2] == 0, 0.0, left[...])
            east = jnp.where(border[3] == 0, 0.0, right[...])
            padded = jnp.concatenate([west, own_ref[...], east], axis=2)
            tapered = jnp.dot(
                padded.reshape(members * pixel_rows, 3 * pixel_cols),
                band_ref[...],
                precision=lax.Precision.HIGHEST,
            )
            values = -0.5 * tapered.reshape(members, pixel_rows, pixel_cols)
            peak = jnp.max(values, axis=0)
            scaled = jnp.exp(values - peak[None])
            total = jnp.sum(scaled, axis=0)
            scaled_ref[...] = scaled
            norm_ref[0] = peak
            norm_ref[1] = total
            store_doubled(share, scaled / total[None])

        for block in range(blocks):
            window = slice(block * LANES, (block + 1) * LANES)
            for level in range(chunk):
                mean = share[0, block] * prior[0, level, :, window].astype(jnp.float32)
                for member in range(1, members):
                    mean = mean + share[member, block] * prior[member, level, :, window].astype(
                        jnp.float32
                    )
                mean_ref[level, :, window] = mean
        for piece in range(pieces):

            @pl.when((step >= piece * per_piece) & (step < (piece + 1) * per_piece))
            def _(piece=piece):
                sent[piece][...] = mean_ref[...].astype(jnp.bfloat16)

    def whole(shape):
        return pl.BlockSpec(shape, lambda i, n=len(shape): (0,) * n)

    def piece_spec(piece):
        return pl.BlockSpec(
            (chunk, rows, cols),
            lambda i: (jnp.clip(i - piece * per_piece, 0, per_piece - 1), 0, 0),
        )

    norm = (2, pixel_rows, pixel_cols)
    return pl.pallas_call(
        kernel,
        grid=(heights // chunk,),
        out_shape=(
            jax.ShapeDtypeStruct(smooth.shape, jnp.float32),
            jax.ShapeDtypeStruct(norm, jnp.float32),
            jax.ShapeDtypeStruct((heights, rows, cols), jnp.float32),
        )
        + (jax.ShapeDtypeStruct((heights // pieces, rows, cols), jnp.bfloat16),) * pieces,
        in_specs=[
            pl.BlockSpec(memory_space=pltpu.SMEM),
            whole(smooth.shape),
            whole(smooth.shape),
            whole(smooth.shape),
            whole(band.shape),
            pl.BlockSpec((members, chunk, rows, cols), lambda i: (0, i, 0, 0)),
        ],
        out_specs=(
            whole(smooth.shape),
            whole(norm),
            pl.BlockSpec((chunk, rows, cols), lambda i: (i, 0, 0)),
        )
        + tuple(piece_spec(piece) for piece in range(pieces)),
        scratch_shapes=[pltpu.VMEM((members, blocks, rows, LANES), jnp.float32)],
        compiler_params=pltpu.CompilerParams(vmem_limit_bytes=16 << 20),
        name="group_mean",
    )(borders, smooth, from_west, from_east, band, prior_states)


def merge(scaled, own_norm, other_norm, shared):
    _, pixel_rows, pixel_cols = scaled.shape

    def kernel(scaled_ref, own_ref, other_ref, weights, parts):
        own_peak, own_total = own_ref[0], own_ref[1]
        other_peak, other_total = other_ref[0], other_ref[1]
        peak = jnp.maximum(own_peak, other_peak)
        own_scale = jnp.exp(own_peak - peak)
        own_part = own_total * own_scale
        if shared:
            total = other_total
            weighted = jnp.stack([jnp.ones_like(total), jnp.zeros_like(total)])
        else:
            other_part = other_total * jnp.exp(other_peak - peak)
            total = own_part + other_part
            weighted = jnp.stack([own_part, other_part]) / total[None]
        store_doubled(parts, (1.0 - relax_factor) * weighted)
        weights[...] = scaled_ref[...] * (own_scale / total)[None]

    return pl.pallas_call(
        kernel,
        out_shape=(
            jax.ShapeDtypeStruct(scaled.shape, jnp.float32),
            jax.ShapeDtypeStruct((2, 2 * pixel_cols // LANES, 2 * pixel_rows, LANES), jnp.float32),
        ),
        name="merge",
    )(scaled, own_norm, other_norm)


def combine(table, parts, own_mean, other_mean, prior_states, received, analysis, first, chunk):
    members, heights, rows, cols = prior_states.shape
    tiles = tiles_of(rows, cols)
    count = len(tiles)
    sources, seats = received.shape[:2]
    received = received.reshape((sources * seats,) + received.shape[2:])
    steps = other_mean.shape[0] // chunk
    start = first // chunk
    done = () if analysis is None else (analysis,)

    def kernel(lookup, parts_ref, mean_ref, peer_ref, prior, remote, *refs):
        out, base = refs[len(done) :]
        for block in range(cols // LANES):
            window = slice(block * LANES, (block + 1) * LANES)
            for level in range(chunk):
                base[level, :, window] = parts_ref[0, block] * mean_ref[
                    level, :, window
                ] + parts_ref[1, block] * peer_ref[level, :, window].astype(jnp.float32)

        def fill(array, source, slot, tile):
            north, east = tiles[tile]
            down = slice(north * PATCH_NORTHWARD, (north + 1) * PATCH_NORTHWARD)
            along = slice(east * PATCH_EASTWARD, (east + 1) * PATCH_EASTWARD)
            for level in range(chunk):
                out[slot, level, down, along] = base[level, down, along] + relax_factor * array[
                    source, level, down, along
                ].astype(jnp.float32)

        for slot in range(members):
            for tile in range(count):
                source = lookup[slot * count + tile]

                @pl.when(source < members)
                def _(slot=slot, tile=tile, source=source):
                    fill(prior, source, slot, tile)

                @pl.when(source >= members)
                def _(slot=slot, tile=tile, source=source):
                    fill(remote, source - members, slot, tile)

    return pl.pallas_call(
        kernel,
        grid=(steps,),
        out_shape=jax.ShapeDtypeStruct(prior_states.shape, jnp.float32),
        in_specs=[
            pl.BlockSpec(memory_space=pltpu.SMEM),
            pl.BlockSpec(parts.shape, lambda i: (0, 0, 0, 0)),
            pl.BlockSpec((chunk, rows, cols), lambda i: (start + i, 0, 0)),
            pl.BlockSpec((chunk, rows, cols), lambda i: (i, 0, 0)),
            pl.BlockSpec((members, chunk, rows, cols), lambda i: (0, start + i, 0, 0)),
            pl.BlockSpec((sources * seats, chunk, rows, cols), lambda i: (0, start + i, 0, 0)),
        ]
        + [pl.BlockSpec(memory_space=pltpu.HBM)] * len(done),
        out_specs=pl.BlockSpec((members, chunk, rows, cols), lambda i: (0, start + i, 0, 0)),
        input_output_aliases={6: 0} if done else {},
        scratch_shapes=[pltpu.VMEM((chunk, rows, cols), jnp.float32)],
        compiler_params=pltpu.CompilerParams(vmem_limit_bytes=24 << 20),
        name="combine",
    )(table, parts, own_mean, other_mean, prior_states, received, *done)


SLOTS = 3


def entry_layer(ancestors, place, prior_states, even_taps, odd_taps, targets, seats):
    members, heights, rows, cols = prior_states.shape
    tiles = tiles_of(rows, cols)
    count = len(tiles)
    groups = ancestors.shape[0] // (members * count)
    channels = odd_taps.shape[0] // 2
    padded = even_taps.shape[1] // 5
    pixel_rows, pixel_cols = rows // 2, cols // 2

    def kernel(
        ancestor, spot, prior, even_ref, odd_ref, field, out, east_ref, west_ref, picked, table,
        sorted_cells, lines, east, west, buffer, used, seen, sems,
    ):
        def transfer(target, seat, member, tile, leaving):
            window = tile_window(*tiles[tile])
            here = buffer.at[(target, seat, slice(None)) + window]
            sem = sems.at[int(leaving), target, seat, tile]
            if leaving:
                away = picked.at[(target, seat, slice(None)) + window]
                return pltpu.make_async_copy(here, away, sem)
            return pltpu.make_async_copy(field.at[(member, slice(None)) + window], here, sem)

        def each_seat(action):
            for target in range(targets):
                for tile in range(count):
                    for seat in range(seats):

                        @pl.when(seat < used[target * count + tile])
                        def _(target=target, tile=tile, seat=seat):
                            action(target, seat, tile)

        def load_then_send(target, seat, tile):
            transfer(target, seat, 0, tile, False).wait()
            transfer(target, seat, 0, tile, True).start()

        @pl.when(pl.program_id(0) == 0)
        def _():
            own = spot[0]
            for target in range(targets):
                for tile in range(count):
                    rank = jnp.int32(0)
                    for slot in range(members):
                        parent = ancestor[(spot[1 + target] * members + slot) * count + tile]
                        local = parent - own * members
                        hit = (local >= 0) & (local < members) & (rank < seats)

                        @pl.when(hit)
                        def _(target=target, rank=rank, local=local, tile=tile):
                            transfer(target, rank, local, tile, False).start()

                        rank = rank + hit.astype(jnp.int32)
                    used[target * count + tile] = rank
            for tile in range(count):
                for group in range(groups):
                    seen[group] = 0
                for slot in range(members):
                    parent = ancestor[(own * members + slot) * count + tile]
                    group = lax.div(parent, jnp.int32(members))
                    rank = seen[group]
                    seen[group] = rank + 1
                    line = (jnp.int32(0) if targets == 1 else group) * seats + rank
                    table[slot * count + tile] = jnp.where(
                        group == own, parent - own * members, members + line
                    )
            lines[...] = jnp.zeros_like(lines)

        @pl.when(pl.program_id(0) == members // 2)
        def _():
            each_seat(load_then_send)

        @pl.when(pl.program_id(0) == members - 1)
        def _():
            each_seat(lambda target, seat, tile: transfer(target, seat, 0, tile, True).wait())

        here = lax.broadcasted_iota(jnp.int32, (cols, cols), 0)
        there = lax.broadcasted_iota(jnp.int32, (cols, cols), 1)
        chosen = jnp.where(there < pixel_cols, 2 * there, 2 * (there - pixel_cols) + 1)
        parity = (here == chosen).astype(jnp.float32).astype(jnp.bfloat16)
        split = jnp.dot(
            prior[0].reshape(heights * rows, cols), parity, preferred_element_type=jnp.float32
        )
        for kind in range(2):
            sorted_cells[kind] = split[:, kind * pixel_cols : (kind + 1) * pixel_cols]
        for kind in range(2):
            for row in range(rows):
                lines[kind, row + 4, :heights] = sorted_cells[
                    kind, pl.ds(row, heights, stride=rows), :
                ].astype(jnp.bfloat16)
        east[...] = jnp.zeros_like(east)
        west[...] = jnp.zeros_like(west)
        lane = lax.broadcasted_iota(jnp.int32, (channels, pixel_cols), 1)
        last = pixel_cols - 1

        def window(kind, row):
            return lines[kind, 2 * row + 2 : 2 * row + 7].reshape(5 * padded, pixel_cols)

        for pair in range(-1, pixel_rows + 1, 2):
            even, odd = (
                jnp.dot(
                    taps[...],
                    jnp.concatenate([window(kind, pair), window(kind, pair + 1)], axis=1),
                    preferred_element_type=jnp.float32,
                )
                for kind, taps in ((0, even_ref), (1, odd_ref))
            )
            for half in range(2):
                row = pair + half
                here_even = even[:, half * pixel_cols : (half + 1) * pixel_cols]
                here_odd = odd[:, half * pixel_cols : (half + 1) * pixel_cols]
                ahead = pltpu.roll(here_even[:channels] + here_odd[:channels], 1, 1)
                behind = pltpu.roll(here_even[2 * channels :], last, 1)
                inside = (
                    here_even[channels : 2 * channels]
                    + here_odd[channels:]
                    + jnp.where(lane == 0, 0.0, ahead)
                    + jnp.where(lane == last, 0.0, behind)
                )
                out[0, row + 1] = inside
                at = 3 * (row + 2)
                onward = pltpu.roll(jnp.where(lane == 0, ahead, inside), at + 2, 1)
                east[...] = jnp.where((lane >= at) & (lane < at + 3), onward, east[...])
                onward = pltpu.roll(jnp.where(lane == last, behind, inside), 65 + at, 1)
                west[...] = jnp.where((lane >= 64 + at) & (lane < 67 + at), onward, west[...])
        east_ref[0] = east[...].astype(jnp.bfloat16)
        west_ref[0] = west[...].astype(jnp.bfloat16)

    sent = (targets, seats, heights, rows, cols)
    edge = jax.ShapeDtypeStruct((members, channels, pixel_cols), jnp.bfloat16)
    edge_spec = pl.BlockSpec((1, channels, pixel_cols), lambda i: (i, 0, 0))
    return pl.pallas_call(
        kernel,
        grid=(members,),
        out_shape=(
            pltpu.HBM((members, pixel_rows + 2, channels, pixel_cols), jnp.float32),
            edge,
            edge,
            jax.ShapeDtypeStruct(sent, prior_states.dtype),
            jax.ShapeDtypeStruct((members * count,), jnp.int32),
        ),
        in_specs=[
            pl.BlockSpec(memory_space=pltpu.SMEM),
            pl.BlockSpec(memory_space=pltpu.SMEM),
            pl.BlockSpec((1, heights, rows, cols), lambda i: (i, 0, 0, 0)),
            pl.BlockSpec(even_taps.shape, lambda i: (0, 0)),
            pl.BlockSpec(odd_taps.shape, lambda i: (0, 0)),
            pl.BlockSpec(memory_space=pltpu.HBM),
        ],
        out_specs=(
            pl.BlockSpec((1, pixel_rows + 2, channels, pixel_cols), lambda i: (i, 0, 0, 0)),
            edge_spec,
            edge_spec,
            pl.BlockSpec(memory_space=pltpu.HBM),
            pl.BlockSpec(memory_space=pltpu.SMEM),
        ),
        scratch_shapes=[
            pltpu.VMEM((2, heights * rows, pixel_cols), jnp.float32),
            pltpu.VMEM((2, rows + 8, padded, pixel_cols), jnp.bfloat16),
            pltpu.VMEM((channels, pixel_cols), jnp.float32),
            pltpu.VMEM((channels, pixel_cols), jnp.float32),
            pltpu.VMEM(sent, prior_states.dtype),
            pltpu.SMEM((targets * count,), jnp.int32),
            pltpu.SMEM((groups,), jnp.int32),
            pltpu.SemaphoreType.DMA((2, targets, seats, count)),
        ],
        compiler_params=pltpu.CompilerParams(vmem_limit_bytes=28 << 20),
        name="entry_layer",
    )(ancestors, place, prior_states, even_taps, odd_taps, prior_states)


def received_sides(from_west, from_east, border):
    west = jnp.where(border[2] == 0, 0.0, from_west.astype(jnp.float32))
    east = jnp.where(border[3] == 0, 0.0, from_east.astype(jnp.float32))
    return west, east


def end_fix(west, east, lane):
    return jnp.where(lax.rem(lane, 3) == 2, west, pltpu.roll(east, 65, 1))


def with_ends(values, fix, row, lane):
    moved = pltpu.roll(fix, (128 - 3 * (row + 2) - 2) % 128, 1)
    return values + jnp.where((lane == 0) | (lane == 127), moved, 0.0)


def side_columns(west, east, own_east, own_west, lane):
    spill = jnp.where(
        lane < 64,
        pltpu.roll(own_west.astype(jnp.float32), 65, 1),
        pltpu.roll(own_east.astype(jnp.float32), 63, 1),
    )
    middle = lax.rem(lax.rem(lane, 64), 3) == 1
    return jnp.where(lane < 64, west, east) + jnp.where(middle, spill, 0.0)


def row_ends(borders, partial, own_east, own_west, from_west, from_east):
    members, row_count, channels, pixel_cols = partial.shape
    tail = row_count // SLOTS - 1

    def kernel(border, top, bottom, own_e, own_w, left, right, north, south):
        lane = lax.broadcasted_iota(jnp.int32, (channels, pixel_cols), 1)
        for member in range(members):
            west, east = received_sides(left[member], right[member], border)
            fix = end_fix(west, east, lane)
            sides = side_columns(west, east, own_e[member], own_w[member], lane)
            for slot in range(SLOTS):
                north[member, slot] = with_ends(top[member, slot], fix, slot - 1, lane).astype(
                    jnp.bfloat16
                )
                south[member, slot] = with_ends(
                    bottom[member, slot], fix, row_count - 4 + slot, lane
                ).astype(jnp.bfloat16)
            north[member, SLOTS] = sides.astype(jnp.bfloat16)
            south[member, SLOTS] = sides.astype(jnp.bfloat16)

    edge_spec = pl.BlockSpec((members, channels, pixel_cols), lambda i: (0, 0, 0))
    rows_spec = (members, SLOTS, channels, pixel_cols)
    sent = (members, SLOTS + 1, channels, pixel_cols)
    return pl.pallas_call(
        kernel,
        grid=(1,),
        out_shape=(jax.ShapeDtypeStruct(sent, jnp.bfloat16),) * 2,
        in_specs=[
            pl.BlockSpec(memory_space=pltpu.SMEM),
            pl.BlockSpec(rows_spec, lambda i: (0, 0, 0, 0)),
            pl.BlockSpec(rows_spec, lambda i: (0, tail, 0, 0)),
            edge_spec,
            edge_spec,
            edge_spec,
            edge_spec,
        ],
        out_specs=(pl.BlockSpec(sent, lambda i: (0, 0, 0, 0)),) * 2,
        compiler_params=pltpu.CompilerParams(vmem_limit_bytes=16 << 20),
        name="row_ends",
    )(borders, partial, partial, own_east, own_west, from_west, from_east)


def misfits(borders, partial, sides, rows_in, inner, fixed):
    members, row_count, channels, pixel_cols = partial.shape
    pixel_rows = row_count - 2
    bands = fixed[2].shape[0]
    edge = SLOTS
    whole_rows = rows_in is None
    if whole_rows:
        wanted = list(range(edge, pixel_rows - edge))
        needed = range(edge - 2, pixel_rows - edge + 2)
    else:
        wanted = [*range(edge), *range(pixel_rows - edge, pixel_rows)]
        needed = [*range(-2, edge + 2), *range(pixel_rows - edge - 2, pixel_rows + 2)]

    def kernel(*refs):
        border, pre, own_e, own_w, left, right = refs[:6]
        refs = refs[6:]
        if not whole_rows:
            above, below, inner_ref = refs[:3]
            refs = refs[3:]
        vectors, weight, matrix_ref, obs, mask_ref = refs[:5]
        out, hidden, taps, side = refs[5:]

        @pl.when(pl.program_id(0) == 0)
        def _():
            for down in range(3):
                line = slice(down * channels, (down + 1) * channels)
                for along in range(3):
                    part = weight[down, along]
                    taps[along * channels : (along + 1) * channels, line] = part
                    if along != 1:
                        half = along // 2 * channels
                        side[half : half + channels, line] = part

        lane = lax.broadcasted_iota(jnp.int32, (channels, pixel_cols), 1)
        bias = jnp.broadcast_to(vectors[:, 0:1], (channels, pixel_cols))
        bias_two = jnp.broadcast_to(vectors[:, 1:2], (channels, pixel_cols))
        offset = jnp.broadcast_to(vectors[:bands, 2:3], (bands, pixel_cols))
        variance = jnp.broadcast_to(vectors[:bands, 3:4], (bands, pixel_cols))
        top, bottom = border[0] == 0, border[1] == 0
        start, end = border[2] == 0, border[3] == 0
        west, east = received_sides(left[0], right[0], border)
        fix = end_fix(west, east, lane)

        for row in needed:
            if row == -2:
                values = above[0, 0].astype(jnp.float32)
            elif row == pixel_rows + 1:
                values = below[0, SLOTS - 1].astype(jnp.float32)
            else:
                values = with_ends(pre[0, row + 1], fix, row, lane)
                if row <= 0:
                    values = values + above[0, row + 2].astype(jnp.float32)
                if row >= pixel_rows - 1:
                    values = values + below[0, row - pixel_rows + 1].astype(jnp.float32)
            values = jnp.maximum(values + bias, 0.0)
            if row < 0:
                values = jnp.where(top, 0.0, values)
            if row >= pixel_rows:
                values = jnp.where(bottom, 0.0, values)
            hidden[row + 2] = values.astype(jnp.bfloat16)

        slot = lax.div(lax.rem(lane, 64), 3)
        cells = side_columns(west, east, own_e[0], own_w[0], lane)
        outside = (start & (lane < 64)) | (end & (lane >= 64))
        if not whole_rows:
            upper = pltpu.roll(above[0, SLOTS].astype(jnp.float32), 128 - 3 * pixel_rows, 1)
            lower = pltpu.roll(below[0, SLOTS].astype(jnp.float32), 3 * pixel_rows, 1)
            cells = (
                cells
                + jnp.where(slot < 3, upper, 0.0)
                + jnp.where((slot > pixel_rows) & (slot < pixel_rows + 4), lower, 0.0)
            )
            outside = outside | (top & (slot < 2)) | (bottom & (slot >= pixel_rows + 2))
        cells = jnp.where(outside, 0.0, jnp.maximum(cells + bias, 0.0))
        stack = jnp.concatenate(
            [pltpu.roll(cells, 6, 1), cells, pltpu.roll(cells, 122, 1)], axis=0
        ).astype(jnp.bfloat16)
        found = jnp.dot(side[...], stack, preferred_element_type=jnp.float32)
        column = jnp.where(lane < 64, found[:channels], found[channels:])

        def window(row):
            return jnp.concatenate([hidden[row], hidden[row + 2], hidden[row + 4]], axis=0)

        if not whole_rows:
            out[0, edge : pixel_rows - edge] = inner_ref[0, edge : pixel_rows - edge]
        for first, second in zip(wanted[::2], wanted[1::2]):
            both = jnp.dot(
                taps[...],
                jnp.concatenate([window(first), window(second)], axis=1),
                preferred_element_type=jnp.float32,
            )
            ready = []
            for half, row in enumerate((first, second)):
                parts = both[:, half * pixel_cols : (half + 1) * pixel_cols]
                at = 3 * (row + 2)
                values = (
                    parts[channels : 2 * channels]
                    + jnp.where(
                        lane < 2,
                        pltpu.roll(column, 128 - at, 1),
                        pltpu.roll(parts[:channels], 2, 1),
                    )
                    + jnp.where(
                        lane >= 126,
                        pltpu.roll(column, (189 - at) % 128, 1),
                        pltpu.roll(parts[2 * channels :], 126, 1),
                    )
                )
                ready.append(jnp.maximum(values + bias_two, 0.0).astype(jnp.bfloat16))
            predicted = jnp.dot(
                matrix_ref[...],
                jnp.concatenate(ready, axis=1),
                preferred_element_type=jnp.float32,
            )
            for half, row in enumerate((first, second)):
                misfit = obs[pl.ds(row, bands, stride=pixel_rows), :] - (
                    predicted[:, half * pixel_cols : (half + 1) * pixel_cols] + offset
                )
                total = jnp.sum(misfit * misfit / variance, axis=0, keepdims=True)
                out[0, row : row + 1] = total * mask_ref[row : row + 1].astype(jnp.float32)

    edge_spec = pl.BlockSpec((1, channels, pixel_cols), lambda i: (i, 0, 0))
    line_spec = pl.BlockSpec((1, SLOTS + 1, channels, pixel_cols), lambda i: (i, 0, 0, 0))
    out_spec = pl.BlockSpec((1, pixel_rows, pixel_cols), lambda i: (i, 0, 0))

    def whole(array):
        return pl.BlockSpec(array.shape, lambda i, n=array.ndim: (0,) * n)

    extra = () if whole_rows else (*rows_in, inner)
    extra_specs = [] if whole_rows else [line_spec, line_spec, out_spec]
    return pl.pallas_call(
        kernel,
        grid=(members,),
        out_shape=jax.ShapeDtypeStruct((members, pixel_rows, pixel_cols), jnp.float32),
        in_specs=[
            pl.BlockSpec(memory_space=pltpu.SMEM),
            pl.BlockSpec((1, row_count, channels, pixel_cols), lambda i: (i, 0, 0, 0)),
        ]
        + [edge_spec] * 4
        + extra_specs
        + [whole(array) for array in fixed],
        out_specs=out_spec,
        scratch_shapes=[
            pltpu.VMEM((pixel_rows + 4, channels, pixel_cols), jnp.bfloat16),
            pltpu.VMEM((3 * channels, 3 * channels), jnp.bfloat16),
            pltpu.VMEM((2 * channels, 3 * channels), jnp.bfloat16),
        ],
        compiler_params=pltpu.CompilerParams(vmem_limit_bytes=16 << 20),
        name="inner_misfits" if whole_rows else "outer_misfits",
    )(borders, partial, *sides, *extra, *fixed)


def neighbours(axis):
    count = lax.axis_size(axis)
    onward = [(i, i + 1) for i in range(count - 1)]
    return onward, [(j, i) for i, j in onward]


def departures(
    ancestors,
    place,
    targets,
    seats,
    prior_states,
    measured_brightness,
    measured_indicator,
    sensor_error_spread,
    entry_layer_stencil,
    entry_layer_offset,
    middle_layer_stencil,
    middle_layer_offset,
    brightness_matrix,
    brightness_offset,
):
    channels, heights = entry_layer_stencil.shape[:2]
    padded = (heights + 15) // 16 * 16
    entry = jnp.pad(entry_layer_stencil, ((0, 0), (0, padded - heights), (0, 0), (0, 0)))
    entry = jnp.transpose(entry, (3, 0, 2, 1)).reshape(5, channels, 5 * padded)
    even_taps = jnp.concatenate([entry[0], entry[2], entry[4]])
    odd_taps = jnp.concatenate([entry[1], entry[3]])
    lat, lon = lax.axis_index("lat"), lax.axis_index("lon")
    borders = jnp.stack(
        [lat, lax.axis_size("lat") - 1 - lat, lon, lax.axis_size("lon") - 1 - lon]
    ).astype(jnp.int32)
    partial, own_east, own_west, picked, table = entry_layer(
        ancestors,
        place,
        pltpu.with_memory_space_constraint(prior_states, pltpu.HBM),
        even_taps,
        odd_taps,
        targets,
        seats,
    )
    partial = pltpu.with_memory_space_constraint(partial, pltpu.HBM)
    count = lax.axis_size("lon")
    ring = [(i, (i + 1) % count) for i in range(count)]
    from_west = lax.ppermute(own_east, "lon", ring)
    from_east = lax.ppermute(own_west, "lon", [(j, i) for i, j in ring])
    sides = (own_east, own_west, from_west, from_east)
    north, south = row_ends(borders, partial, *sides)
    onward, back = neighbours("lat")
    from_north = lax.ppermute(south, "lat", onward)
    from_south = lax.ppermute(north, "lat", back)
    bands = brightness_matrix.shape[0]
    vectors = jnp.stack(
        [
            entry_layer_offset,
            middle_layer_offset,
            jnp.pad(brightness_offset, (0, channels - bands)),
            jnp.pad(sensor_error_spread, (0, channels - bands), constant_values=1.0),
        ],
        axis=1,
    )
    fixed = (
        vectors,
        jnp.transpose(middle_layer_stencil, (2, 3, 0, 1)),
        brightness_matrix,
        measured_brightness.reshape(-1, measured_brightness.shape[-1]),
        measured_indicator,
    )
    inner = misfits(borders, partial, sides, None, None, fixed)
    squares = misfits(borders, partial, sides, (from_north, from_south), inner, fixed)
    return squares, picked, table, borders


def chunk_of(heights):
    return next(size for size in (5, 4, 2, 1) if heights % size == 0)


def body(prior_states, *rest):
    ancestor_indices = rest[-1]
    members, heights, rows, cols = prior_states.shape
    groups = lax.axis_size("ens")
    own = lax.axis_index("ens").astype(jnp.int32)
    seats = max(2, (members + groups - 1) // groups)
    ancestors = ancestor_indices.reshape(-1)
    swap = [(0, 1), (1, 0)]
    paired = groups == 2
    if paired:
        targets = (1 - own)[None]
    else:
        targets = jnp.arange(groups, dtype=jnp.int32)
    place = jnp.concatenate([own[None], targets])
    squares, picked, table, borders = departures(
        ancestors, place, targets.shape[0], seats, prior_states, *rest[:-1]
    )
    if paired:
        received = lax.ppermute(picked, "ens", swap)
    else:
        received = lax.all_to_all(picked, "ens", split_axis=0, concat_axis=0, tiled=True)
    band_lat = taper_band(squares.shape[1], RADIUS)
    padded = extended(squares, (("lat", 1),), RADIUS)
    smooth = jnp.einsum("ij,pjk->pik", band_lat, padded, precision=lax.Precision.HIGHEST)
    pixel_cols = squares.shape[2]
    band_lon = np.zeros((3 * pixel_cols, pixel_cols), np.float32)
    near = slice(pixel_cols - RADIUS, 2 * pixel_cols + RADIUS)
    band_lon[near] = taper_band(pixel_cols, RADIUS).T
    count = lax.axis_size("lon")
    ring = [(i, (i + 1) % count) for i in range(count)]
    from_west = lax.ppermute(smooth, "lon", ring)
    from_east = lax.ppermute(smooth, "lon", [(j, i) for i, j in ring])
    size = chunk_of(heights)
    pieces = PIECES if heights // size % PIECES == 0 else 1
    levels = heights // pieces
    field = prior_states
    scaled, own_norm, own_mean, *sent = group_mean(
        borders, smooth, from_west, from_east, band_lon, field, pieces, size
    )
    if paired:
        other_norm = lax.ppermute(own_norm, "ens", swap)
        others = [lax.ppermute(piece, "ens", swap) for piece in sent]
    else:
        peak = lax.pmax(own_norm[0], "ens")
        part = own_norm[1] * jnp.exp(own_norm[0] - peak)
        total, added = lax.psum((part, expand_patches(part)[None] * own_mean), "ens")
        own_mean = added / expand_patches(total)[None]
        other_norm = jnp.stack([peak, total])
        others = sent
    weights, parts = merge(scaled, own_norm, other_norm, not paired)
    analysis = None
    for k, other_mean in enumerate(others):
        analysis = combine(
            table, parts, own_mean, other_mean, field, received, analysis, k * levels, size
        )
    return analysis, weights


def solution(mesh):
    return jax.shard_map(
        body,
        mesh=mesh,
        in_specs=(
            P("ens", None, "lat", "lon"),
            P(None, "lat", "lon"),
            P("lat", "lon"),
            P(),
            P(),
            P(),
            P(),
            P(),
            P(),
            P(),
            P(None, "lat", "lon"),
        ),
        out_specs=(P("ens", None, "lat", "lon"), P("ens", "lat", "lon")),
        check_vma=False,
    )
```

profile of v0, /device:TPU:0, one launch (start us, length us, event | category | flops | bytes accessed | tf_op | source)
XLA Modules:
  0.0 104.5 jit_solution(17468394418423213008)
XLA Ops:
  0.6 0.8 copy.38
  1.4 0.1 reshape.27.ancestor
  1.5 1.0 pad_bitcast_fusion
  2.5 0.1 copy.42
  2.6 0.1 copy.43
  2.7 0.1 copy.41
  2.8 0.1 copy.40
  2.9 0.1 copy.39
  3.0 0.1 pad_add_fusion.spot
  3.1 21.3 %entry_layer.1 = (f32[8,18,64,128]{3,2,1,0:T(8,128)}, bf16[8,64,128]{2,1,0:T(8,128)(2,1)S(1)}, bf16[8,64,128]{2,1,0:T(8,128)(2,1)S(1)}, bf16[1,4,40,32,256]{4,3,2,1,0:T(8,128)(2,1)}, s32[16]{0:T(128)S(1)}) custom-call(s32[32]{0:T(128)S(1)} %reshape.27.ancestor, s32[2]{0:T(128)S(1)} %pad_add_fusion.spot, bf16[8,40,32,256]{3,2,1,0:T(8,128)(2,1)} %prior.11, ...), custom_call_target="tpu_custom_call" | custom-call | tf_op jit(solution)/shard_map/entry_layer/pallas_call | solution.py:392
  24.5 3.0 %collective-permute-start.10 = (bf16[1,4,40,32,256]{4,3,2,1,0:T(8,128)(2,1)}, bf16[1,4,40,32,256]{4,3,2,1,0:T(8,128)(2,1)}, u32[]{:S(2)}, u32[]{:S(2)}) collective-permute-start(bf16[1,4,40,32,256]{4,3,2,1,0:T(8,128)(2,1)} %get-tuple-element.29), channel_id=1, source_target_pairs={{0,16},{16,0},{1,17},{17,1},{2,18},{18,2},{3,19},{19,3},{4,20},{20... | collective-permute-start | bytes 7864328 | tf_op jit(solution)/shard_map/ppermute | solution.py:746
  27.5 1.7 %collective-permute-start.1 = (bf16[8,64,128]{2,1,0:T(8,128)(2,1)S(1)}, bf16[8,64,128]{2,1,0:T(8,128)(2,1)S(1)}, u32[]{:S(2)}, u32[]{:S(2)}) collective-permute-start(bf16[8,64,128]{2,1,0:T(8,128)(2,1)S(1)} %get-tuple-element.21.own_w.refs_3_), channel_id=1, source_target_pairs={{1,0},{2,1},{3,2},{0,3},{5,4},{6,5},{7,6},{4,7},{9,8},{10,9},{11,1... | collective-permute-start | bytes 393224 | tf_op jit(solution)/shard_map/ppermute | solution.py:696
  29.3 0.1 pad_add_fusion.1.border.refs_0_
  29.4 2.6 %collective-permute-done.left.refs_4_ = bf16[8,64,128]{2,1,0:T(8,128)(2,1)S(1)} collective-permute-done((bf16[8,64,128]{2,1,0:T(8,128)(2,1)S(1)}, bf16[8,64,128]{2,1,0:T(8,128)(2,1)S(1)}, u32[]{:S(2)}, u32[]{:S(2)}) %collective-permute-start) | collective-permute-done | bytes 131104 | tf_op jit(solution)/shard_map/ppermute | solution.py:695
  31.9 0.4 collective-permute-done.1.right.refs_5_
  32.4 3.0 %row_ends.1 = (bf16[8,4,64,128]{3,2,1,0:T(8,128)(2,1)S(1)}, bf16[8,4,64,128]{3,2,1,0:T(8,128)(2,1)}) custom-call(s32[4]{0:T(128)S(1)} %pad_add_fusion.1.border.refs_0_, f32[8,18,64,128]{3,2,1,0:T(8,128)} %get-tuple-element.19.top.bottom.refs_1_, f32[8,18,64,128]{3,2,1,0:T(8,128)} %get-tuple-element.19.top.bottom.refs_1_, ...), custom_call_target="tpu_custom_call" | custom-call | tf_op jit(solution)/shard_map/row_ends/pallas_call | solution.py:480
  35.4 3.5 %collective-permute-start.2 = (bf16[8,4,64,128]{3,2,1,0:T(8,128)(2,1)}, bf16[8,4,64,128]{3,2,1,0:T(8,128)(2,1)S(1)}, u32[]{:S(2)}, u32[]{:S(2)}) collective-permute-start(bf16[8,4,64,128]{3,2,1,0:T(8,128)(2,1)} %get-tuple-element.22), channel_id=1, source_target_pairs={{0,4},{4,8},{8,12},{1,5},{5,9},{9,13},{2,6},{6,10},{10,14},{3,7},{... | collective-permute-start | bytes 1572872 | tf_op jit(solution)/shard_map/ppermute | solution.py:700
  38.9 1.3 %collective-permute-start.3 = (bf16[8,4,64,128]{3,2,1,0:T(8,128)(2,1)S(1)}, bf16[8,4,64,128]{3,2,1,0:T(8,128)(2,1)S(1)}, u32[]{:S(2)}, u32[]{:S(2)}) collective-permute-start(bf16[8,4,64,128]{3,2,1,0:T(8,128)(2,1)S(1)} %get-tuple-element.23), channel_id=1, source_target_pairs={{4,0},{8,4},{12,8},{5,1},{9,5},{13,9},{6,2},{10,6},{14,10},{7,3},{... | collective-permute-start | bytes 1572872 | tf_op jit(solution)/shard_map/ppermute | solution.py:701
  40.3 0.1 copy.44.refs_6_.refs_9_
  40.4 0.0 copy-start.10
  40.4 0.0 slice-start.1
  40.4 12.4 %inner_misfits.1.refs_8_ = f32[8,16,128]{2,1,0:T(8,128)S(1)} custom-call(s32[4]{0:T(128)S(1)} %pad_add_fusion.1.border.refs_0_, f32[8,18,64,128]{3,2,1,0:T(8,128)} %get-tuple-element.19.top.bottom.refs_1_, bf16[8,64,128]{2,1,0:T(8,128)(2,1)S(1)} %get-tuple-element.20.own_e.refs_2_, bf16[8,64,128]{2,1,0:T(8,128)(2,1)S(1)} %get-tuple-element.21.own_w.refs_3_, ...), custom_call_target="tpu_custom_call" | custom-call | tf_op jit(solution)/shard_map/inner_misfits/pallas_call | solution.py:629
  52.8 2.4 %collective-permute-done.3.refs_7_ = bf16[8,4,64,128]{3,2,1,0:T(8,128)(2,1)S(1)} collective-permute-done((bf16[8,4,64,128]{3,2,1,0:T(8,128)(2,1)S(1)}, bf16[8,4,64,128]{3,2,1,0:T(8,128)(2,1)S(1)}, u32[]{:S(2)}, u32[]{:S(2)}) %collective-permute-start.3) | collective-permute-done | bytes 524320 | tf_op jit(solution)/shard_map/ppermute | solution.py:701
  55.3 9.3 %outer_misfits.1 = f32[8,16,128]{2,1,0:T(8,128)S(1)} custom-call(s32[4]{0:T(128)S(1)} %pad_add_fusion.1.border.refs_0_, f32[8,18,64,128]{3,2,1,0:T(8,128)} %get-tuple-element.19.top.bottom.refs_1_, bf16[8,64,128]{2,1,0:T(8,128)(2,1)S(1)} %get-tuple-element.20.own_e.refs_2_, bf16[8,64,128]{2,1,0:T(8,128)(2,1)S(1)} %get-tuple-element.21.own_w.refs_3_, ...), custom_call_target="tpu_custom_call" | custom-call | tf_op jit(solution)/shard_map/outer_misfits/pallas_call | solution.py:629
  64.5 1.3 %collective-permute-start.5 = (f32[8,16,128]{2,1,0:T(8,128)S(1)}, f32[8,16,128]{2,1,0:T(8,128)S(1)}, u32[]{:S(2)}, u32[]{:S(2)}) collective-permute-start(f32[8,16,128]{2,1,0:T(8,128)S(1)} %outer_misfits.1), channel_id=1, source_target_pairs={{4,0},{8,4},{12,8},{5,1},{9,5},{13,9},{6,2},{10,6},{14,10},{7,3},{... | collective-permute-start | bytes 196616 | tf_op jit(solution)/shard_map/ppermute | solution.py:26
  65.8 4.5 %collective-permute-start.4 = (f32[8,16,128]{2,1,0:T(8,128)S(1)}, f32[8,16,128]{2,1,0:T(8,128)S(1)}, u32[]{:S(2)}, u32[]{:S(2)}) collective-permute-start(f32[8,16,128]{2,1,0:T(8,128)S(1)} %outer_misfits.1), channel_id=1, source_target_pairs={{0,4},{4,8},{8,12},{1,5},{5,9},{9,13},{2,6},{6,10},{10,14},{3,7},{... | collective-permute-start | bytes 196616 | tf_op jit(solution)/shard_map/ppermute | solution.py:25
  70.4 0.6 collective-permute-done.5
  71.0 1.3 %collective-permute-done.4 = f32[8,16,128]{2,1,0:T(8,128)S(1)} collective-permute-done((f32[8,16,128]{2,1,0:T(8,128)S(1)}, f32[8,16,128]{2,1,0:T(8,128)S(1)}, u32[]{:S(2)}, u32[]{:S(2)}) %collective-permute-start.4) | collective-permute-done | bytes 65568 | tf_op jit(solution)/shard_map/ppermute | solution.py:25
  72.3 0.2 convolution_bitcast_fusion.own_ref
  72.5 0.2 collective-permute-start.7
  72.8 0.3 collective-permute-start.6
  73.1 1.6 %collective-permute-done.7.right = f32[8,16,128]{2,1,0:T(8,128)S(1)} collective-permute-done((f32[8,16,128]{2,1,0:T(8,128)S(1)}, f32[8,16,128]{2,1,0:T(8,128)S(1)}, u32[]{:S(2)}, u32[]{:S(2)}) %collective-permute-start.7) | collective-permute-done | bytes 65568 | tf_op jit(solution)/shard_map/ppermute | solution.py:759
  74.7 2.3 %collective-permute-done.6.left = f32[8,16,128]{2,1,0:T(8,128)S(1)} collective-permute-done((f32[8,16,128]{2,1,0:T(8,128)S(1)}, f32[8,16,128]{2,1,0:T(8,128)S(1)}, u32[]{:S(2)}, u32[]{:S(2)}) %collective-permute-start.6) | collective-permute-done | bytes 65568 | tf_op jit(solution)/shard_map/ppermute | solution.py:758
  77.0 3.0 %group_mean.1 = (f32[8,16,128]{2,1,0:T(8,128)S(1)}, f32[2,16,128]{2,1,0:T(8,128)S(1)}, f32[40,32,256]{2,1,0:T(8,128)S(1)}, bf16[10,32,256]{2,1,0:T(8,128)(2,1)S(...) custom-call(s32[4]{0:T(128)S(1)} %pad_add_fusion.1.border.refs_0_, ...), custom_call_target="tpu_custom_call" | custom-call | tf_op jit(solution)/shard_map/group_mean/pallas_call | solution.py:141
  80.0 0.6 copy-done.5
  80.7 0.6 collective-permute-start.8
  81.2 1.5 %collective-permute-start.13 = (bf16[10,32,256]{2,1,0:T(8,128)(2,1)S(1)}, bf16[10,32,256]{2,1,0:T(8,128)(2,1)S(1)}, u32[]{:S(2)}, u32[]{:S(2)}) collective-permute-start(bf16[10,32,256]{2,1,0:T(8,128)(2,1)S(1)} %get-tuple-element.32), channel_id=1, source_target_pairs={{0,16},{16,0},{1,17},{17,1},{2,18},{18,2},{3,19},{19,3},{4,20},{20... | collective-permute-start | bytes 491528 | tf_op jit(solution)/shard_map/ppermute | solution.py:769
  82.7 0.6 collective-permute-start.12
  83.3 1.5 %collective-permute-start.11 = (bf16[10,32,256]{2,1,0:T(8,128)(2,1)S(1)}, bf16[10,32,256]{2,1,0:T(8,128)(2,1)S(1)}, u32[]{:S(2)}, u32[]{:S(2)}) collective-permute-start(bf16[10,32,256]{2,1,0:T(8,128)(2,1)S(1)} %get-tuple-element.30), channel_id=1, source_target_pairs={{0,16},{16,0},{1,17},{17,1},{2,18},{18,2},{3,19},{19,3},{4,20},{20... | collective-permute-start | bytes 491528 | tf_op jit(solution)/shard_map/ppermute | solution.py:769
  84.7 1.1 %collective-permute-done.8.other_ref = f32[2,16,128]{2,1,0:T(8,128)S(1)} collective-permute-done((f32[2,16,128]{2,1,0:T(8,128)S(1)}, f32[2,16,128]{2,1,0:T(8,128)S(1)}, u32[]{:S(2)}, u32[]{:S(2)}) %collective-permute-start.8) | collective-permute-done | bytes 16416 | tf_op jit(solution)/shard_map/ppermute | solution.py:768
  85.8 2.1 %collective-permute-start.9 = (bf16[10,32,256]{2,1,0:T(8,128)(2,1)S(1)}, bf16[10,32,256]{2,1,0:T(8,128)(2,1)S(1)}, u32[]{:S(2)}, u32[]{:S(2)}) collective-permute-start(bf16[10,32,256]{2,1,0:T(8,128)(2,1)S(1)} %get-tuple-element.28), channel_id=1, source_target_pairs={{0,16},{16,0},{1,17},{17,1},{2,18},{18,2},{3,19},{19,3},{4,20},{20... | collective-permute-start | bytes 491528 | tf_op jit(solution)/shard_map/ppermute | solution.py:769
  87.9 1.7 %merge.1 = (f32[8,16,128]{2,1,0:T(8,128)}, f32[2,2,32,128]{3,2,1,0:T(8,128)}) custom-call(f32[8,16,128]{2,1,0:T(8,128)} %copy-done.5, f32[2,16,128]{2,1,0:T(8,128)} %copy-done.8, f32[2,16,128]{2,1,0:T(8,128)} %copy-done.9), custom_call_target="tpu_custom_call" | custom-call | tf_op jit(solution)/shard_map/merge/pallas_call | solution.py:189
  89.5 2.5 %copy-done = bf16[8,40,32,256]{3,2,1,0:T(8,128)(2,1)S(1)} copy-done((bf16[8,40,32,256]{3,2,1,0:T(8,128)(2,1)S(1)}, bf16[8,40,32,256]{3,2,1,0:T(8,128)(2,1)}, u32[]{:S(2)}) %copy-start) | copy-done | bytes 5242904
  92.0 0.8 copy-done.1
  92.9 2.9 %combine.4.refs_0_ = f32[8,40,32,256]{3,2,1,0:T(8,128)} custom-call(s32[16]{0:T(128)S(1)} %get-tuple-element.18.lookup, f32[2,2,32,128]{3,2,1,0:T(8,128)S(1)} %copy-done.1, f32[40,32,256]{2,1,0:T(8,128)S(1)} %get-tuple-element.27.mean_ref, bf16[10,32,256]{2,1,0:T(8,128)(2,1)S(1)} %collective-permute-done.13.peer_ref, bf16[8,40,32,256]{3,2,1,0:T(8,128)(2,1)S(1)} %copy-done, ...), custom_call_target="tpu_custom_call" | custom-call | tf_op jit(solution)/shard_map/combine/pallas_call | solution.py:239
  95.8 2.9 %combine.5.refs_0_ = f32[8,40,32,256]{3,2,1,0:T(8,128)} custom-call(s32[16]{0:T(128)S(1)} %get-tuple-element.18.lookup, f32[2,2,32,128]{3,2,1,0:T(8,128)S(1)} %copy-done.1, f32[40,32,256]{2,1,0:T(8,128)S(1)} %get-tuple-element.27.mean_ref, bf16[10,32,256]{2,1,0:T(8,128)(2,1)S(1)} %collective-permute-done.12.peer_ref, ...), custom_call_target="tpu_custom_call", output_to_operand_aliasing={{}: (6, {})} | custom-call | tf_op jit(solution)/shard_map/combine/pallas_call | solution.py:239
  98.7 2.9 %combine.6.refs_0_ = f32[8,40,32,256]{3,2,1,0:T(8,128)} custom-call(s32[16]{0:T(128)S(1)} %get-tuple-element.18.lookup, f32[2,2,32,128]{3,2,1,0:T(8,128)S(1)} %copy-done.1, f32[40,32,256]{2,1,0:T(8,128)S(1)} %get-tuple-element.27.mean_ref, bf16[10,32,256]{2,1,0:T(8,128)(2,1)S(1)} %collective-permute-done.11.peer_ref, ...), custom_call_target="tpu_custom_call", output_to_operand_aliasing={{}: (6, {})} | custom-call | tf_op jit(solution)/shard_map/combine/pallas_call | solution.py:239
  101.6 2.9 %combine.7 = f32[8,40,32,256]{3,2,1,0:T(8,128)} custom-call(s32[16]{0:T(128)S(1)} %get-tuple-element.18.lookup, f32[2,2,32,128]{3,2,1,0:T(8,128)S(1)} %copy-done.1, f32[40,32,256]{2,1,0:T(8,128)S(1)} %get-tuple-element.27.mean_ref, bf16[10,32,256]{2,1,0:T(8,128)(2,1)S(1)} %collective-permute-done.9.peer_ref, ...), custom_call_target="tpu_custom_call", output_to_operand_aliasing={{}: (6, {})} | custom-call | tf_op jit(solution)/shard_map/combine/pallas_call | solution.py:239
  (42 shorter events, 0.2 us)
Async XLA Ops:
  24.4 15.8 %copy-start.11 = (f32[16]{0:T(128)S(1)}, f32[16]{0:T(128)}, u32[]{:S(2)}) copy-start(f32[16]{0:T(128)} %param.16) | copy-start | bytes 196
  24.4 15.8 %copy-start.12 = (f32[16]{0:T(128)S(1)}, f32[16]{0:T(128)}, u32[]{:S(2)}) copy-start(f32[16]{0:T(128)} %param.22) | copy-start | bytes 196
  24.4 15.8 %copy-start.13 = (f32[64]{0:T(128)S(1)}, f32[64]{0:T(128)}, u32[]{:S(2)}) copy-start(f32[64]{0:T(128)} %param.20) | copy-start | bytes 772
  24.5 15.8 %copy-start.14 = (f32[64]{0:T(128)S(1)}, f32[64]{0:T(128)}, u32[]{:S(2)}) copy-start(f32[64]{0:T(128)} %param.18) | copy-start | bytes 772
  24.5 15.9 %copy-start.2 = (bf16[64,64,3,3]{1,0,3,2:T(8,128)(2,1)S(1)}, bf16[64,64,3,3]{1,0,3,2:T(8,128)(2,1)}, u32[]{:S(2)}) copy-start(bf16[64,64,3,3]{1,0,3,2:T(8,128)(2,1)} %param.19) | copy-start | bytes 221188
  24.5 15.9 %copy-start.3 = (f32[16,16,128]{2,1,0:T(8,128)S(1)}, f32[16,16,128]{2,1,0:T(8,128)}, u32[]{:S(2)}) copy-start(f32[16,16,128]{2,1,0:T(8,128)} %param.14) | copy-start | bytes 393220
  24.5 15.9 %copy-start.6 = (s32[16,128]{1,0:T(8,128)S(1)}, s32[16,128]{1,0:T(8,128)}, u32[]{:S(2)}) copy-start(s32[16,128]{1,0:T(8,128)} %refs_13_.1) | copy-start | bytes 24580
  24.5 15.9 %copy-start.7 = (bf16[16,64]{1,0:T(8,128)(2,1)S(1)}, bf16[16,64]{1,0:T(8,128)(2,1)}, u32[]{:S(2)}) copy-start(bf16[16,64]{1,0:T(8,128)(2,1)} %refs_11_.1) | copy-start | bytes 6148
  24.5 65.0 %collective-permute-start.10 = (bf16[1,4,40,32,256]{4,3,2,1,0:T(8,128)(2,1)}, bf16[1,4,40,32,256]{4,3,2,1,0:T(8,128)(2,1)}, u32[]{:S(2)}, u32[]{:S(2)}) collective-permute-start(bf16[1,4,40,32,256]{4,3,2,1,0:T(8,128)(2,1)} %get-tuple-element.29), channel_id=1, source_target_pairs={{0,16},{16,0},{1,17},{17,1},{2,18},{18,2},{3,19},{19,3},{4,20},{20... | collective-permute-start | bytes 7864328 | tf_op jit(solution)/shard_map/ppermute | solution.py:746
  27.5 4.4 %collective-permute-start = (bf16[8,64,128]{2,1,0:T(8,128)(2,1)S(1)}, bf16[8,64,128]{2,1,0:T(8,128)(2,1)S(1)}, u32[]{:S(2)}, u32[]{:S(2)}) collective-permute-start(bf16[8,64,128]{2,1,0:T(8,128)(2,1)S(1)} %get-tuple-element.20.own_e.refs_2_), channel_id=1, source_target_pairs={{0,1},{1,2},{2,3},{3,0},{4,5},{5,6},{6,7},{7,4},{8,9},{9,10},{10,1... | collective-permute-start | bytes 393224 | tf_op jit(solution)/shard_map/ppermute | solution.py:695
  27.5 4.8 %collective-permute-start.1 = (bf16[8,64,128]{2,1,0:T(8,128)(2,1)S(1)}, bf16[8,64,128]{2,1,0:T(8,128)(2,1)S(1)}, u32[]{:S(2)}, u32[]{:S(2)}) collective-permute-start(bf16[8,64,128]{2,1,0:T(8,128)(2,1)S(1)} %get-tuple-element.21.own_w.refs_3_), channel_id=1, source_target_pairs={{1,0},{2,1},{3,2},{0,3},{5,4},{6,5},{7,6},{4,7},{9,8},{10,9},{11,1... | collective-permute-start | bytes 393224 | tf_op jit(solution)/shard_map/ppermute | solution.py:696
  32.4 44.6 %slice-start = ((s8[5242880]{0:T(1024)(128)(4,1)}), s8[1048576]{0:T(1024)(128)(4,1)S(1)}, s32[]{:S(2)}) async-start(s8[5242880]{0:T(1024)(128)(4,1)} %bitcast.28), calls=%async_computation | async-start | bytes 2097152
  35.4 17.4 %collective-permute-start.2 = (bf16[8,4,64,128]{3,2,1,0:T(8,128)(2,1)}, bf16[8,4,64,128]{3,2,1,0:T(8,128)(2,1)S(1)}, u32[]{:S(2)}, u32[]{:S(2)}) collective-permute-start(bf16[8,4,64,128]{3,2,1,0:T(8,128)(2,1)} %get-tuple-element.22), channel_id=1, source_target_pairs={{0,4},{4,8},{8,12},{1,5},{5,9},{9,13},{2,6},{6,10},{10,14},{3,7},{... | collective-permute-start | bytes 1572872 | tf_op jit(solution)/shard_map/ppermute | solution.py:700
  38.9 16.3 %collective-permute-start.3 = (bf16[8,4,64,128]{3,2,1,0:T(8,128)(2,1)S(1)}, bf16[8,4,64,128]{3,2,1,0:T(8,128)(2,1)S(1)}, u32[]{:S(2)}, u32[]{:S(2)}) collective-permute-start(bf16[8,4,64,128]{3,2,1,0:T(8,128)(2,1)S(1)} %get-tuple-element.23), channel_id=1, source_target_pairs={{4,0},{8,4},{12,8},{5,1},{9,5},{13,9},{6,2},{10,6},{14,10},{7,3},{... | collective-permute-start | bytes 1572872 | tf_op jit(solution)/shard_map/ppermute | solution.py:701
  40.4 31.9 %copy-start.10 = (f32[16,48,1]{1,0,2:T(8,128)S(1)}, f32[16,48,1]{1,0,2:T(8,128)}, u32[]{:S(2)}) copy-start(f32[16,48,1]{1,0,2:T(8,128)} %constant.37) | copy-start | bytes 9220
  40.4 36.6 %slice-start.1 = ((s8[5242880]{0:T(1024)(128)(4,1)}), s8[4194304]{0:T(1024)(128)(4,1)S(1)}, s32[]{:S(2)}) async-start(s8[5242880]{0:T(1024)(128)(4,1)} %bitcast.28), calls=%async_computation.1 | async-start | bytes 8388608
  40.4 36.6 %copy-start.4 = (f32[384,128]{1,0:T(8,128)S(1)}, f32[384,128]{1,0:T(8,128)}, u32[]{:S(2)}) copy-start(f32[384,128]{1,0:T(8,128)} %constant.29.clone.band_ref) | copy-start | bytes 589828
  64.5 6.5 %collective-permute-start.5 = (f32[8,16,128]{2,1,0:T(8,128)S(1)}, f32[8,16,128]{2,1,0:T(8,128)S(1)}, u32[]{:S(2)}, u32[]{:S(2)}) collective-permute-start(f32[8,16,128]{2,1,0:T(8,128)S(1)} %outer_misfits.1), channel_id=1, source_target_pairs={{4,0},{8,4},{12,8},{5,1},{9,5},{13,9},{6,2},{10,6},{14,10},{7,3},{... | collective-permute-start | bytes 196616 | tf_op jit(solution)/shard_map/ppermute | solution.py:26
  65.8 6.4 %collective-permute-start.4 = (f32[8,16,128]{2,1,0:T(8,128)S(1)}, f32[8,16,128]{2,1,0:T(8,128)S(1)}, u32[]{:S(2)}, u32[]{:S(2)}) collective-permute-start(f32[8,16,128]{2,1,0:T(8,128)S(1)} %outer_misfits.1), channel_id=1, source_target_pairs={{0,4},{4,8},{8,12},{1,5},{5,9},{9,13},{2,6},{6,10},{10,14},{3,7},{... | collective-permute-start | bytes 196616 | tf_op jit(solution)/shard_map/ppermute | solution.py:25
  72.5 2.2 %collective-permute-start.7 = (f32[8,16,128]{2,1,0:T(8,128)S(1)}, f32[8,16,128]{2,1,0:T(8,128)S(1)}, u32[]{:S(2)}, u32[]{:S(2)}) collective-permute-start(f32[8,16,128]{2,1,0:T(8,128)S(1)} %convolution_bitcast_fusion.own_ref), channel_id=1, source_target_pairs={{1,0},{2,1},{3,2},{0,3},{5,4},{6,5},{7,6},{4,7},{9,8},{10,9},{11,1... | collective-permute-start | bytes 196616 | tf_op jit(solution)/shard_map/ppermute | solution.py:759
  72.8 4.2 %collective-permute-start.6 = (f32[8,16,128]{2,1,0:T(8,128)S(1)}, f32[8,16,128]{2,1,0:T(8,128)S(1)}, u32[]{:S(2)}, u32[]{:S(2)}) collective-permute-start(f32[8,16,128]{2,1,0:T(8,128)S(1)} %convolution_bitcast_fusion.own_ref), channel_id=1, source_target_pairs={{0,1},{1,2},{2,3},{3,0},{4,5},{5,6},{6,7},{7,4},{8,9},{9,10},{10,1... | collective-permute-start | bytes 196616 | tf_op jit(solution)/shard_map/ppermute | solution.py:758
  80.0 0.6 copy-start.5
  80.7 7.2 %copy-start.8 = (f32[2,16,128]{2,1,0:T(8,128)}, f32[2,16,128]{2,1,0:T(8,128)S(1)}, u32[]{:S(2)}) copy-start(f32[2,16,128]{2,1,0:T(8,128)S(1)} %get-tuple-element.25.own_ref) | copy-start | bytes 49156
  80.7 5.1 %collective-permute-start.8 = (f32[2,16,128]{2,1,0:T(8,128)S(1)}, f32[2,16,128]{2,1,0:T(8,128)S(1)}, u32[]{:S(2)}, u32[]{:S(2)}) collective-permute-start(f32[2,16,128]{2,1,0:T(8,128)S(1)} %get-tuple-element.25.own_ref), channel_id=1, source_target_pairs={{0,16},{16,0},{1,17},{17,1},{2,18},{18,2},{3,19},{19,3},{4,20},{20... | collective-permute-start | bytes 49160 | tf_op jit(solution)/shard_map/ppermute | solution.py:768
  81.2 8.3 %collective-permute-start.13 = (bf16[10,32,256]{2,1,0:T(8,128)(2,1)S(1)}, bf16[10,32,256]{2,1,0:T(8,128)(2,1)S(1)}, u32[]{:S(2)}, u32[]{:S(2)}) collective-permute-start(bf16[10,32,256]{2,1,0:T(8,128)(2,1)S(1)} %get-tuple-element.32), channel_id=1, source_target_pairs={{0,16},{16,0},{1,17},{17,1},{2,18},{18,2},{3,19},{19,3},{4,20},{20... | collective-permute-start | bytes 491528 | tf_op jit(solution)/shard_map/ppermute | solution.py:769
  82.7 13.0 %collective-permute-start.12 = (bf16[10,32,256]{2,1,0:T(8,128)(2,1)S(1)}, bf16[10,32,256]{2,1,0:T(8,128)(2,1)S(1)}, u32[]{:S(2)}, u32[]{:S(2)}) collective-permute-start(bf16[10,32,256]{2,1,0:T(8,128)(2,1)S(1)} %get-tuple-element.31), channel_id=1, source_target_pairs={{0,16},{16,0},{1,17},{17,1},{2,18},{18,2},{3,19},{19,3},{4,20},{20... | collective-permute-start | bytes 491528 | tf_op jit(solution)/shard_map/ppermute | solution.py:769
  83.3 15.4 %collective-permute-start.11 = (bf16[10,32,256]{2,1,0:T(8,128)(2,1)S(1)}, bf16[10,32,256]{2,1,0:T(8,128)(2,1)S(1)}, u32[]{:S(2)}, u32[]{:S(2)}) collective-permute-start(bf16[10,32,256]{2,1,0:T(8,128)(2,1)S(1)} %get-tuple-element.30), channel_id=1, source_target_pairs={{0,16},{16,0},{1,17},{17,1},{2,18},{18,2},{3,19},{19,3},{4,20},{20... | collective-permute-start | bytes 491528 | tf_op jit(solution)/shard_map/ppermute | solution.py:769
  85.8 2.1 %copy-start.9 = (f32[2,16,128]{2,1,0:T(8,128)}, f32[2,16,128]{2,1,0:T(8,128)S(1)}, u32[]{:S(2)}) copy-start(f32[2,16,128]{2,1,0:T(8,128)S(1)} %collective-permute-done.8.other_ref) | copy-start | bytes 49156
  85.8 15.8 %collective-permute-start.9 = (bf16[10,32,256]{2,1,0:T(8,128)(2,1)S(1)}, bf16[10,32,256]{2,1,0:T(8,128)(2,1)S(1)}, u32[]{:S(2)}, u32[]{:S(2)}) collective-permute-start(bf16[10,32,256]{2,1,0:T(8,128)(2,1)S(1)} %get-tuple-element.28), channel_id=1, source_target_pairs={{0,16},{16,0},{1,17},{17,1},{2,18},{18,2},{3,19},{19,3},{4,20},{20... | collective-permute-start | bytes 491528 | tf_op jit(solution)/shard_map/ppermute | solution.py:769
  89.5 2.5 %copy-start = (bf16[8,40,32,256]{3,2,1,0:T(8,128)(2,1)S(1)}, bf16[8,40,32,256]{3,2,1,0:T(8,128)(2,1)}, u32[]{:S(2)}) copy-start(bf16[8,40,32,256]{3,2,1,0:T(8,128)(2,1)} %prior.11) | copy-start | bytes 15728644
  92.0 0.8 copy-start.1
where the time goes:
time: 105 us
  Pallas kernels  62.2 us (59%)
  starting transfers between devices  22.1 us (21%)
  waiting for transfers between devices  12.3 us (12%)
  local copies, waits for them, and re-layouts  6.45 us (6%)
    pallas_call x2, Pallas kernels, misfits(): pl.pallas_call(kernel, grid=(members,), out_shape=jax.ShapeDtypeStruct((m...  21.6 us
    pallas_call x1, Pallas kernels, entry_layer(): pl.pallas_call(kernel, grid=(members,), out_shape=(pltpu.HBM((members, pi...  21.3 us
    pallas_call x4, Pallas kernels, combine(): pl.pallas_call(kernel, grid=(steps,), out_shape=jax.ShapeDtypeStruct(prio...  11.6 us
    ppermute x4, starting transfers between devices, body(): others = [lax.ppermute(piece, 'ens', swap) for piece in sent]  5.56 us
    unnamed x35, local copies, waits for them, and re-layouts  4.78 us
    ppermute x1, starting transfers between devices, extended(): before = lax.ppermute(last, axis, up)  4.55 us
    ppermute x1, starting transfers between devices, departures(): from_north = lax.ppermute(south, 'lat', onward)  3.51 us
    ppermute x1, starting transfers between devices, body(): received = lax.ppermute(picked, 'ens', swap)  3.03 us
  transfers between devices with their start and end apart: 14, of which 8 were waited for; matrix products, arithmetic and copies ran while one was open for 0% of the time, Pallas kernels for 36%

commit v1 on v0

--- a/solution.py
+++ b/solution.py
@@ -1,3 +1,5 @@
+import math
+
 import jax
 import jax.numpy as jnp
 from jax import lax
@@ -47,6 +49,10 @@
 
 
 LANES = 128
+
+
+def held(array):
+    return pltpu.with_memory_space_constraint(array, pltpu.HBM)
 
 
 def store_doubled(out, values):
@@ -142,8 +148,8 @@
         kernel,
         grid=(heights // chunk,),
         out_shape=(
-            jax.ShapeDtypeStruct(smooth.shape, jnp.float32),
-            jax.ShapeDtypeStruct(norm, jnp.float32),
+            pltpu.HBM(smooth.shape, jnp.float32),
+            pltpu.HBM(norm, jnp.float32),
             jax.ShapeDtypeStruct((heights, rows, cols), jnp.float32),
         )
         + (jax.ShapeDtypeStruct((heights // pieces, rows, cols), jnp.bfloat16),) * pieces,
@@ -190,10 +196,10 @@
         kernel,
         out_shape=(
             jax.ShapeDtypeStruct(scaled.shape, jnp.float32),
-            jax.ShapeDtypeStruct((2, 2 * pixel_cols // LANES, 2 * pixel_rows, LANES), jnp.float32),
+            pltpu.HBM((2, 2 * pixel_cols // LANES, 2 * pixel_rows, LANES), jnp.float32),
         ),
         name="merge",
-    )(scaled, own_norm, other_norm)
+    )(held(scaled), held(own_norm), other_norm)
 
 
 def combine(table, parts, own_mean, other_mean, prior_states, received, analysis, first, chunk):
@@ -207,7 +213,17 @@
     done = () if analysis is None else (analysis,)
 
     def kernel(lookup, parts_ref, mean_ref, peer_ref, prior, remote, *refs):
-        out, base = refs[len(done) :]
+        analysis_ref, out, base, sems = refs[len(done) :]
+        step = pl.program_id(0)
+        half = lax.rem(step, 2)
+
+        def leave(at, slot, which):
+            return pltpu.make_async_copy(
+                out.at[which, slot],
+                analysis_ref.at[slot, pl.ds(first + at * chunk, chunk)],
+                sems.at[which, slot],
+            )
+
         for block in range(cols // LANES):
             window = slice(block * LANES, (block + 1) * LANES)
             for level in range(chunk):
@@ -220,11 +236,16 @@
             down = slice(north * PATCH_NORTHWARD, (north + 1) * PATCH_NORTHWARD)
             along = slice(east * PATCH_EASTWARD, (east + 1) * PATCH_EASTWARD)
             for level in range(chunk):
-                out[slot, level, down, along] = base[level, down, along] + relax_factor * array[
+                out[half, slot, level, down, along] = base[level, down, along] + relax_factor * array[
                     source, level, down, along
                 ].astype(jnp.float32)
 
         for slot in range(members):
+
+            @pl.when(step >= 2)
+            def _(slot=slot):
+                leave(step - 2, slot, half).wait()
+
             for tile in range(count):
                 source = lookup[slot * count + tile]
 
@@ -235,6 +256,15 @@
                 @pl.when(source >= members)
                 def _(slot=slot, tile=tile, source=source):
                     fill(remote, source - members, slot, tile)
+
+            leave(step, slot, half).start()
+
+        @pl.when(step == steps - 1)
+        def _():
+            for slot in range(members):
+                if steps > 1:
+                    leave(step - 1, slot, 1 - half).wait()
+                leave(step, slot, half).wait()
 
     return pl.pallas_call(
         kernel,
@@ -249,29 +279,34 @@
             pl.BlockSpec((sources * seats, chunk, rows, cols), lambda i: (0, start + i, 0, 0)),
         ]
         + [pl.BlockSpec(memory_space=pltpu.HBM)] * len(done),
-        out_specs=pl.BlockSpec((members, chunk, rows, cols), lambda i: (0, start + i, 0, 0)),
+        out_specs=pl.BlockSpec(memory_space=pltpu.HBM),
         input_output_aliases={6: 0} if done else {},
-        scratch_shapes=[pltpu.VMEM((chunk, rows, cols), jnp.float32)],
-        compiler_params=pltpu.CompilerParams(vmem_limit_bytes=24 << 20),
+        scratch_shapes=[
+            pltpu.VMEM((2, members, chunk, rows, cols), jnp.float32),
+            pltpu.VMEM((chunk, rows, cols), jnp.float32),
+            pltpu.SemaphoreType.DMA((2, members)),
+        ],
+        compiler_params=pltpu.CompilerParams(vmem_limit_bytes=12 << 20),
         name="combine",
-    )(table, parts, own_mean, other_mean, prior_states, received, *done)
+    )(table, held(parts), own_mean, other_mean, held(prior_states), held(received), *done)
 
 
 SLOTS = 3
-
-
-def entry_layer(ancestors, place, prior_states, even_taps, odd_taps, targets, seats):
+PACKED = 4
+
+
+def entry_layer(ancestors, place, prior_states, weights, targets, seats):
     members, heights, rows, cols = prior_states.shape
     tiles = tiles_of(rows, cols)
     count = len(tiles)
-    groups = ancestors.shape[0] // (members * count)
-    channels = odd_taps.shape[0] // 2
-    padded = even_taps.shape[1] // 5
+    groups = ancestors.shape[1] // members
+    channels = weights.shape[-1]
+    padded = pl.cdiv(heights, 16) * 16
     pixel_rows, pixel_cols = rows // 2, cols // 2
 
     def kernel(
-        ancestor, spot, prior, even_ref, odd_ref, field, out, east_ref, west_ref, picked, table,
-        sorted_cells, lines, east, west, buffer, used, seen, sems,
+        ancestor, spot, prior, weight, field, out, east_ref, west_ref, picked, table,
+        sorted_cells, lines, even_ref, odd_ref, east, west, buffer, used, seen, sems,
     ):
         def transfer(target, seat, member, tile, leaving):
             window = tile_window(*tiles[tile])
@@ -302,7 +337,7 @@
                 for tile in range(count):
                     rank = jnp.int32(0)
                     for slot in range(members):
-                        parent = ancestor[(spot[1 + target] * members + slot) * count + tile]
+                        parent = ancestor[tile, spot[1 + target] * members + slot]
                         local = parent - own * members
                         hit = (local >= 0) & (local < members) & (rank < seats)
 
@@ -316,7 +351,7 @@
                 for group in range(groups):
                     seen[group] = 0
                 for slot in range(members):
-                    parent = ancestor[(own * members + slot) * count + tile]
+                    parent = ancestor[tile, own * members + slot]
                     group = lax.div(parent, jnp.int32(members))
                     rank = seen[group]
                     seen[group] = rank + 1
@@ -325,6 +360,14 @@
                         group == own, parent - own * members, members + line
                     )
             lines[...] = jnp.zeros_like(lines)
+            even_ref[...] = jnp.zeros_like(even_ref)
+            odd_ref[...] = jnp.zeros_like(odd_ref)
+            for down in range(5):
+                for along in range(5):
+                    part = weight[down, along].astype(jnp.float32).T.astype(jnp.bfloat16)
+                    taps = odd_ref if along % 2 else even_ref
+                    line = along // 2 * channels
+                    taps[line : line + channels, down * padded : down * padded + heights] = part
 
         @pl.when(pl.program_id(0) == members // 2)
         def _():
@@ -396,15 +439,14 @@
             pltpu.HBM((members, pixel_rows + 2, channels, pixel_cols), jnp.float32),
             edge,
             edge,
-            jax.ShapeDtypeStruct(sent, prior_states.dtype),
+            pltpu.HBM(sent, prior_states.dtype),
             jax.ShapeDtypeStruct((members * count,), jnp.int32),
         ),
         in_specs=[
             pl.BlockSpec(memory_space=pltpu.SMEM),
             pl.BlockSpec(memory_space=pltpu.SMEM),
             pl.BlockSpec((1, heights, rows, cols), lambda i: (i, 0, 0, 0)),
-            pl.BlockSpec(even_taps.shape, lambda i: (0, 0)),
-            pl.BlockSpec(odd_taps.shape, lambda i: (0, 0)),
+            pl.BlockSpec(weights.shape, lambda i: (0, 0, 0, 0)),
             pl.BlockSpec(memory_space=pltpu.HBM),
         ],
         out_specs=(
@@ -417,6 +459,8 @@
         scratch_shapes=[
             pltpu.VMEM((2, heights * rows, pixel_cols), jnp.float32),
             pltpu.VMEM((2, rows + 8, padded, pixel_cols), jnp.bfloat16),
+            pltpu.VMEM((3 * channels, 5 * padded), jnp.bfloat16),
+            pltpu.VMEM((2 * channels, 5 * padded), jnp.bfloat16),
             pltpu.VMEM((channels, pixel_cols), jnp.float32),
             pltpu.VMEM((channels, pixel_cols), jnp.float32),
             pltpu.VMEM(sent, prior_states.dtype),
@@ -424,9 +468,11 @@
             pltpu.SMEM((groups,), jnp.int32),
             pltpu.SemaphoreType.DMA((2, targets, seats, count)),
         ],
-        compiler_params=pltpu.CompilerParams(vmem_limit_bytes=28 << 20),
+        compiler_params=pltpu.CompilerParams(
+            vmem_limit_bytes=(12 << 20) + 2 * math.prod(sent)
+        ),
         name="entry_layer",
-    )(ancestors, place, prior_states, even_taps, odd_taps, prior_states)
+    )(ancestors, place, prior_states, weights, prior_states)
 
 
 def received_sides(from_west, from_east, border):
@@ -465,18 +511,24 @@
             fix = end_fix(west, east, lane)
             sides = side_columns(west, east, own_e[member], own_w[member], lane)
             for slot in range(SLOTS):
-                north[member, slot] = with_ends(top[member, slot], fix, slot - 1, lane).astype(
+                north[member * SLOTS + slot] = with_ends(top[member, slot], fix, slot - 1, lane).astype(
                     jnp.bfloat16
                 )
-                south[member, slot] = with_ends(
+                south[member * SLOTS + slot] = with_ends(
                     bottom[member, slot], fix, row_count - 4 + slot, lane
                 ).astype(jnp.bfloat16)
-            north[member, SLOTS] = sides.astype(jnp.bfloat16)
-            south[member, SLOTS] = sides.astype(jnp.bfloat16)
+            line, place = divmod(member, PACKED)
+            shown = lax.rem(lane, 64) // 16 == place
+            for sent_rows, slot in ((north, 1), (south, row_count - 2)):
+                moved = pltpu.roll(sides, (16 * place - 3 * slot) % 128, 1)
+                kept = sent_rows[members * SLOTS + line].astype(jnp.float32) if place else 0.0
+                sent_rows[members * SLOTS + line] = jnp.where(shown, moved, kept).astype(
+                    jnp.bfloat16
+                )
 
     edge_spec = pl.BlockSpec((members, channels, pixel_cols), lambda i: (0, 0, 0))
     rows_spec = (members, SLOTS, channels, pixel_cols)
-    sent = (members, SLOTS + 1, channels, pixel_cols)
+    sent = (members * SLOTS + pl.cdiv(members, PACKED), channels, pixel_cols)
     return pl.pallas_call(
         kernel,
         grid=(1,),
@@ -490,10 +542,13 @@
             edge_spec,
             edge_spec,
         ],
-        out_specs=(pl.BlockSpec(sent, lambda i: (0, 0, 0, 0)),) * 2,
-        compiler_params=pltpu.CompilerParams(vmem_limit_bytes=16 << 20),
+        out_specs=(pl.BlockSpec(sent, lambda i: (0, 0, 0)),) * 2,
+        compiler_params=pltpu.CompilerParams(vmem_limit_bytes=10 << 20),
         name="row_ends",
-    )(borders, partial, partial, own_east, own_west, from_west, from_east)
+    )(
+        borders,
+        held(partial), held(partial), own_east, own_west, from_west, from_east,
+    )
 
 
 def misfits(borders, partial, sides, rows_in, inner, fixed):
@@ -513,8 +568,8 @@
         border, pre, own_e, own_w, left, right = refs[:6]
         refs = refs[6:]
         if not whole_rows:
-            above, below, inner_ref = refs[:3]
-            refs = refs[3:]
+            above, below, above_sides, below_sides, inner_ref = refs[:5]
+            refs = refs[5:]
         vectors, weight, matrix_ref, obs, mask_ref = refs[:5]
         out, hidden, taps, side = refs[5:]
 
@@ -541,15 +596,15 @@
 
         for row in needed:
             if row == -2:
-                values = above[0, 0].astype(jnp.float32)
+                values = above[0].astype(jnp.float32)
             elif row == pixel_rows + 1:
-                values = below[0, SLOTS - 1].astype(jnp.float32)
+                values = below[SLOTS - 1].astype(jnp.float32)
             else:
                 values = with_ends(pre[0, row + 1], fix, row, lane)
                 if row <= 0:
-                    values = values + above[0, row + 2].astype(jnp.float32)
+                    values = values + above[row + 2].astype(jnp.float32)
                 if row >= pixel_rows - 1:
-                    values = values + below[0, row - pixel_rows + 1].astype(jnp.float32)
+                    values = values + below[row - pixel_rows + 1].astype(jnp.float32)
             values = jnp.maximum(values + bias, 0.0)
             if row < 0:
                 values = jnp.where(top, 0.0, values)
@@ -561,8 +616,15 @@
         cells = side_columns(west, east, own_e[0], own_w[0], lane)
         outside = (start & (lane < 64)) | (end & (lane >= 64))
         if not whole_rows:
-            upper = pltpu.roll(above[0, SLOTS].astype(jnp.float32), 128 - 3 * pixel_rows, 1)
-            lower = pltpu.roll(below[0, SLOTS].astype(jnp.float32), 3 * pixel_rows, 1)
+            place = 16 * lax.rem(pl.program_id(0), PACKED)
+            upper = pltpu.roll(
+                above_sides[0].astype(jnp.float32), lax.rem(pixel_cols - place, pixel_cols), 1
+            )
+            lower = pltpu.roll(
+                below_sides[0].astype(jnp.float32), 3 * (pixel_rows + 1) - place + (
+                    0 if 3 * (pixel_rows + 1) >= 16 * (PACKED - 1) else pixel_cols
+                ), 1
+            )
             cells = (
                 cells
                 + jnp.where(slot < 3, upper, 0.0)
@@ -618,14 +680,17 @@
                 out[0, row : row + 1] = total * mask_ref[row : row + 1].astype(jnp.float32)
 
     edge_spec = pl.BlockSpec((1, channels, pixel_cols), lambda i: (i, 0, 0))
-    line_spec = pl.BlockSpec((1, SLOTS + 1, channels, pixel_cols), lambda i: (i, 0, 0, 0))
+    line_spec = pl.BlockSpec((SLOTS, channels, pixel_cols), lambda i: (i, 0, 0))
+    packed_spec = pl.BlockSpec(
+        (1, channels, pixel_cols), lambda i: (members * SLOTS + lax.div(i, PACKED), 0, 0)
+    )
     out_spec = pl.BlockSpec((1, pixel_rows, pixel_cols), lambda i: (i, 0, 0))
 
     def whole(array):
         return pl.BlockSpec(array.shape, lambda i, n=array.ndim: (0,) * n)
 
-    extra = () if whole_rows else (*rows_in, inner)
-    extra_specs = [] if whole_rows else [line_spec, line_spec, out_spec]
+    extra = () if whole_rows else (*rows_in, *rows_in, inner)
+    extra_specs = [] if whole_rows else [line_spec] * 2 + [packed_spec] * 2 + [out_spec]
     return pl.pallas_call(
         kernel,
         grid=(members,),
@@ -643,9 +708,9 @@
             pltpu.VMEM((3 * channels, 3 * channels), jnp.bfloat16),
             pltpu.VMEM((2 * channels, 3 * channels), jnp.bfloat16),
         ],
-        compiler_params=pltpu.CompilerParams(vmem_limit_bytes=16 << 20),
+        compiler_params=pltpu.CompilerParams(vmem_limit_bytes=8 << 20),
         name="inner_misfits" if whole_rows else "outer_misfits",
-    )(borders, partial, *sides, *extra, *fixed)
+    )(borders, held(partial), *sides, *extra, *[held(x) for x in fixed])
 
 
 def neighbours(axis):
@@ -670,12 +735,7 @@
     brightness_matrix,
     brightness_offset,
 ):
-    channels, heights = entry_layer_stencil.shape[:2]
-    padded = (heights + 15) // 16 * 16
-    entry = jnp.pad(entry_layer_stencil, ((0, 0), (0, padded - heights), (0, 0), (0, 0)))
-    entry = jnp.transpose(entry, (3, 0, 2, 1)).reshape(5, channels, 5 * padded)
-    even_taps = jnp.concatenate([entry[0], entry[2], entry[4]])
-    odd_taps = jnp.concatenate([entry[1], entry[3]])
+    channels = entry_layer_stencil.shape[0]
     lat, lon = lax.axis_index("lat"), lax.axis_index("lon")
     borders = jnp.stack(
         [lat, lax.axis_size("lat") - 1 - lat, lon, lax.axis_size("lon") - 1 - lon]
@@ -683,13 +743,11 @@
     partial, own_east, own_west, picked, table = entry_layer(
         ancestors,
         place,
-        pltpu.with_memory_space_constraint(prior_states, pltpu.HBM),
-        even_taps,
-        odd_taps,
+        held(prior_states),
+        held(jnp.transpose(entry_layer_stencil, (2, 3, 1, 0))),
         targets,
         seats,
     )
-    partial = pltpu.with_memory_space_constraint(partial, pltpu.HBM)
     count = lax.axis_size("lon")
     ring = [(i, (i + 1) % count) for i in range(count)]
     from_west = lax.ppermute(own_east, "lon", ring)
@@ -731,7 +789,7 @@
     groups = lax.axis_size("ens")
     own = lax.axis_index("ens").astype(jnp.int32)
     seats = max(2, (members + groups - 1) // groups)
-    ancestors = ancestor_indices.reshape(-1)
+    ancestors = jnp.transpose(ancestor_indices, (1, 2, 0)).reshape(-1, ancestor_indices.shape[0])
     swap = [(0, 1), (1, 0)]
     paired = groups == 2
     if paired:

time: 105 us -> 101 us (0.962)
  local copies, waits for them, and re-layouts: 6.45 us -> 1.44 us
    unnamed x35 -> x20, local copies, waits for them, and re-layouts: 4.78 us -> 0.73 us
    ppermute x1, waiting for transfers between devices: 2.41 us -> 0.01 us  [departures(): from_south = lax.ppermute(north, 'lat', back)]
  transfers between devices with their start and end apart: 14 -> 14, of which waited for: 8 -> 9; matrix products, arithmetic and copies ran while one was open for 0% -> 1% of each run, Pallas kernels for 36% -> 38%
where the time goes in v1:
time: 101 us
  Pallas kernels  62.6 us (62%)
  starting transfers between devices  22.7 us (22%)
  waiting for transfers between devices  12.6 us (12%)
  local copies, waits for them, and re-layouts  1.44 us (1%)
    pallas_call x2, Pallas kernels, misfits(): pl.pallas_call(kernel, grid=(members,), out_shape=jax.ShapeDtypeStruct((m...  21.9 us
    pallas_call x1, Pallas kernels, entry_layer(): pl.pallas_call(kernel, grid=(members,), out_shape=(pltpu.HBM((members, pi...  21.5 us
    pallas_call x4, Pallas kernels, combine(): pl.pallas_call(kernel, grid=(steps,), out_shape=jax.ShapeDtypeStruct(prio...  11.6 us
    ppermute x4, starting transfers between devices, body(): others = [lax.ppermute(piece, 'ens', swap) for piece in sent]  5.57 us
    ppermute x1, starting transfers between devices, extended(): before = lax.ppermute(last, axis, up)  5.18 us
    pallas_call x1, Pallas kernels, group_mean(): pl.pallas_call(kernel, grid=(heights // chunk,), out_shape=(pltpu.HBM(smo...  3.66 us
    ppermute x1, starting transfers between devices, departures(): from_north = lax.ppermute(south, 'lat', onward)  3.51 us
    ppermute x1, starting transfers between devices, body(): received = lax.ppermute(picked, 'ens', swap)  3 us
  transfers between devices with their start and end apart: 14, of which 9 were waited for; matrix products, arithmetic and copies ran while one was open for 1% of the time, Pallas kernels for 38%

profile of v1, /device:TPU:0, one launch (start us, length us, event | category | flops | bytes accessed | tf_op | source)
XLA Modules:
  0.0 100.6 jit_solution(2283305433338458257)
XLA Ops:
  0.6 0.1 pad_add_fusion.spot
  0.7 0.7 copy-done.1
  1.4 21.5 %entry_layer.1 = (f32[8,18,64,128]{3,2,1,0:T(8,128)}, bf16[8,64,128]{2,1,0:T(8,128)(2,1)S(1)}, bf16[8,64,128]{2,1,0:T(8,128)(2,1)S(1)}, bf16[1,4,40,32,256]{4,3,2,1,0:T(8,128)(2,1)}, s32[16]{0:T(128)S(1)}) custom-call(s32[2,16]{1,0:T(2,128)S(1)} %bitcast.25, s32[2]{0:T(128)S(1)} %pad_add_fusion.spot, bf16[8,40,32,256]{3,2,1,0:T(8,128)(2,1)} %prior.11, ...), custom_call_target="tpu_custom_call" | custom-call | tf_op jit(solution)/shard_map/entry_layer/pallas_call | solution.py:435
  22.9 0.0 copy-start.4
  22.9 0.0 copy-start.5
  22.9 0.0 copy-start.6
  22.9 0.0 copy-start.7
  22.9 3.0 %collective-permute-start.10 = (bf16[1,4,40,32,256]{4,3,2,1,0:T(8,128)(2,1)}, bf16[1,4,40,32,256]{4,3,2,1,0:T(8,128)(2,1)}, u32[]{:S(2)}, u32[]{:S(2)}) collective-permute-start(bf16[1,4,40,32,256]{4,3,2,1,0:T(8,128)(2,1)} %get-tuple-element.29), channel_id=1, source_target_pairs={{0,16},{16,0},{1,17},{17,1},{2,18},{18,2},{3,19},{19,3},{4,20},{20... | collective-permute-start | bytes 7864328 | tf_op jit(solution)/shard_map/ppermute | solution.py:804
  26.0 1.7 %collective-permute-start.1 = (bf16[8,64,128]{2,1,0:T(8,128)(2,1)S(1)}, bf16[8,64,128]{2,1,0:T(8,128)(2,1)S(1)}, u32[]{:S(2)}, u32[]{:S(2)}) collective-permute-start(bf16[8,64,128]{2,1,0:T(8,128)(2,1)S(1)} %get-tuple-element.21.own_w.refs_3_), channel_id=1, source_target_pairs={{1,0},{2,1},{3,2},{0,3},{5,4},{6,5},{7,6},{4,7},{9,8},{10,9},{11,1... | collective-permute-start | bytes 393224 | tf_op jit(solution)/shard_map/ppermute | solution.py:754
  27.7 0.1 pad_add_fusion.1.border.refs_0_
  27.8 2.6 %collective-permute-done.left.refs_4_ = bf16[8,64,128]{2,1,0:T(8,128)(2,1)S(1)} collective-permute-done((bf16[8,64,128]{2,1,0:T(8,128)(2,1)S(1)}, bf16[8,64,128]{2,1,0:T(8,128)(2,1)S(1)}, u32[]{:S(2)}, u32[]{:S(2)}) %collective-permute-start) | collective-permute-done | bytes 131104 | tf_op jit(solution)/shard_map/ppermute | solution.py:753
  30.3 0.4 collective-permute-done.1.right.refs_5_
  30.8 2.2 %row_ends.1 = (bf16[26,64,128]{2,1,0:T(8,128)(2,1)S(1)}, bf16[26,64,128]{2,1,0:T(8,128)(2,1)S(1)}) custom-call(s32[4]{0:T(128)S(1)} %pad_add_fusion.1.border.refs_0_, f32[8,18,64,128]{3,2,1,0:T(8,128)} %get-tuple-element.19.top.bottom.refs_1_, f32[8,18,64,128]{3,2,1,0:T(8,128)} %get-tuple-element.19.top.bottom.refs_1_, ...), custom_call_target="tpu_custom_call" | custom-call | tf_op jit(solution)/shard_map/row_ends/pallas_call | solution.py:532
  33.0 3.5 %collective-permute-start.2 = (bf16[26,64,128]{2,1,0:T(8,128)(2,1)S(1)}, bf16[26,64,128]{2,1,0:T(8,128)(2,1)S(1)}, u32[]{:S(2)}, u32[]{:S(2)}) collective-permute-start(bf16[26,64,128]{2,1,0:T(8,128)(2,1)S(1)} %get-tuple-element.22), channel_id=1, source_target_pairs={{0,4},{4,8},{8,12},{1,5},{5,9},{9,13},{2,6},{6,10},{10,14},{3,7},{... | collective-permute-start | bytes 1277960 | tf_op jit(solution)/shard_map/ppermute | solution.py:758
  36.5 1.3 %collective-permute-start.3 = (bf16[26,64,128]{2,1,0:T(8,128)(2,1)S(1)}, bf16[26,64,128]{2,1,0:T(8,128)(2,1)S(1)}, u32[]{:S(2)}, u32[]{:S(2)}) collective-permute-start(bf16[26,64,128]{2,1,0:T(8,128)(2,1)S(1)} %get-tuple-element.23), channel_id=1, source_target_pairs={{4,0},{8,4},{12,8},{5,1},{9,5},{13,9},{6,2},{10,6},{14,10},{7,3},{... | collective-permute-start | bytes 1277960 | tf_op jit(solution)/shard_map/ppermute | solution.py:759
  37.9 0.7 copy.22.refs_6_.refs_11_
  38.6 12.5 %inner_misfits.1.refs_10_ = f32[8,16,128]{2,1,0:T(8,128)S(1)} custom-call(s32[4]{0:T(128)S(1)} %pad_add_fusion.1.border.refs_0_, f32[8,18,64,128]{3,2,1,0:T(8,128)} %get-tuple-element.19.top.bottom.refs_1_, bf16[8,64,128]{2,1,0:T(8,128)(2,1)S(1)} %get-tuple-element.20.own_e.refs_2_, bf16[8,64,128]{2,1,0:T(8,128)(2,1)S(1)} %get-tuple-element.21.own_w.refs_3_, ...), custom_call_target="tpu_custom_call" | custom-call | tf_op jit(solution)/shard_map/inner_misfits/pallas_call | solution.py:694
  51.1 0.0 slice-start.1
  51.1 0.0 copy-start
  51.1 0.0 collective-permute-done.2.refs_6_.refs_8_
  51.1 0.0 collective-permute-done.3.refs_7_.refs_9_
  51.1 9.5 %outer_misfits.1 = f32[8,16,128]{2,1,0:T(8,128)S(1)} custom-call(s32[4]{0:T(128)S(1)} %pad_add_fusion.1.border.refs_0_, f32[8,18,64,128]{3,2,1,0:T(8,128)} %get-tuple-element.19.top.bottom.refs_1_, bf16[8,64,128]{2,1,0:T(8,128)(2,1)S(1)} %get-tuple-element.20.own_e.refs_2_, bf16[8,64,128]{2,1,0:T(8,128)(2,1)S(1)} %get-tuple-element.21.own_w.refs_3_, ...), custom_call_target="tpu_custom_call" | custom-call | tf_op jit(solution)/shard_map/outer_misfits/pallas_call | solution.py:694
  60.6 1.3 %collective-permute-start.5 = (f32[8,16,128]{2,1,0:T(8,128)S(1)}, f32[8,16,128]{2,1,0:T(8,128)S(1)}, u32[]{:S(2)}, u32[]{:S(2)}) collective-permute-start(f32[8,16,128]{2,1,0:T(8,128)S(1)} %outer_misfits.1), channel_id=1, source_target_pairs={{4,0},{8,4},{12,8},{5,1},{9,5},{13,9},{6,2},{10,6},{14,10},{7,3},{... | collective-permute-start | bytes 196616 | tf_op jit(solution)/shard_map/ppermute | solution.py:28
  61.9 5.2 %collective-permute-start.4 = (f32[8,16,128]{2,1,0:T(8,128)S(1)}, f32[8,16,128]{2,1,0:T(8,128)S(1)}, u32[]{:S(2)}, u32[]{:S(2)}) collective-permute-start(f32[8,16,128]{2,1,0:T(8,128)S(1)} %outer_misfits.1), channel_id=1, source_target_pairs={{0,4},{4,8},{8,12},{1,5},{5,9},{9,13},{2,6},{6,10},{10,14},{3,7},{... | collective-permute-start | bytes 196616 | tf_op jit(solution)/shard_map/ppermute | solution.py:27
  67.1 0.7 collective-permute-done.5
  67.8 1.7 %collective-permute-done.4 = f32[8,16,128]{2,1,0:T(8,128)S(1)} collective-permute-done((f32[8,16,128]{2,1,0:T(8,128)S(1)}, f32[8,16,128]{2,1,0:T(8,128)S(1)}, u32[]{:S(2)}, u32[]{:S(2)}) %collective-permute-start.4) | collective-permute-done | bytes 65568 | tf_op jit(solution)/shard_map/ppermute | solution.py:27
  69.5 0.2 convolution_bitcast_fusion.own_ref
  69.7 0.4 collective-permute-start.7
  70.2 0.1 collective-permute-start.6
  70.3 1.8 %collective-permute-done.7.right = f32[8,16,128]{2,1,0:T(8,128)S(1)} collective-permute-done((f32[8,16,128]{2,1,0:T(8,128)S(1)}, f32[8,16,128]{2,1,0:T(8,128)S(1)}, u32[]{:S(2)}, u32[]{:S(2)}) %collective-permute-start.7) | collective-permute-done | bytes 65568 | tf_op jit(solution)/shard_map/ppermute | solution.py:817
  72.1 2.4 %collective-permute-done.6.left = f32[8,16,128]{2,1,0:T(8,128)S(1)} collective-permute-done((f32[8,16,128]{2,1,0:T(8,128)S(1)}, f32[8,16,128]{2,1,0:T(8,128)S(1)}, u32[]{:S(2)}, u32[]{:S(2)}) %collective-permute-start.6) | collective-permute-done | bytes 65568 | tf_op jit(solution)/shard_map/ppermute | solution.py:816
  74.6 3.7 %group_mean.1 = (f32[8,16,128]{2,1,0:T(8,128)}, f32[2,16,128]{2,1,0:T(8,128)}, f32[40,32,256]{2,1,0:T(8,128)S(1)}, bf16[10,32,256]{2,1,0:T(8,128)(2,1)S(1)}, bf1...) custom-call(s32[4]{0:T(128)S(1)} %pad_add_fusion.1.border.refs_0_, ...), custom_call_target="tpu_custom_call" | custom-call | tf_op jit(solution)/shard_map/group_mean/pallas_call | solution.py:147
  78.2 0.5 collective-permute-start.8
  78.8 1.5 %collective-permute-start.13 = (bf16[10,32,256]{2,1,0:T(8,128)(2,1)S(1)}, bf16[10,32,256]{2,1,0:T(8,128)(2,1)S(1)}, u32[]{:S(2)}, u32[]{:S(2)}) collective-permute-start(bf16[10,32,256]{2,1,0:T(8,128)(2,1)S(1)} %get-tuple-element.32), channel_id=1, source_target_pairs={{0,16},{16,0},{1,17},{17,1},{2,18},{18,2},{3,19},{19,3},{4,20},{20... | collective-permute-start | bytes 491528 | tf_op jit(solution)/shard_map/ppermute | solution.py:827
  80.2 0.5 collective-permute-start.12
  80.8 1.5 %collective-permute-start.11 = (bf16[10,32,256]{2,1,0:T(8,128)(2,1)S(1)}, bf16[10,32,256]{2,1,0:T(8,128)(2,1)S(1)}, u32[]{:S(2)}, u32[]{:S(2)}) collective-permute-start(bf16[10,32,256]{2,1,0:T(8,128)(2,1)S(1)} %get-tuple-element.30), channel_id=1, source_target_pairs={{0,16},{16,0},{1,17},{17,1},{2,18},{18,2},{3,19},{19,3},{4,20},{20... | collective-permute-start | bytes 491528 | tf_op jit(solution)/shard_map/ppermute | solution.py:827
  82.3 1.9 %collective-permute-done.8.other_ref = f32[2,16,128]{2,1,0:T(8,128)S(1)} collective-permute-done((f32[2,16,128]{2,1,0:T(8,128)}, f32[2,16,128]{2,1,0:T(8,128)S(1)}, u32[]{:S(2)}, u32[]{:S(2)}) %collective-permute-start.8) | collective-permute-done | bytes 16416 | tf_op jit(solution)/shard_map/ppermute | solution.py:826
  84.2 2.1 %collective-permute-start.9 = (bf16[10,32,256]{2,1,0:T(8,128)(2,1)S(1)}, bf16[10,32,256]{2,1,0:T(8,128)(2,1)S(1)}, u32[]{:S(2)}, u32[]{:S(2)}) collective-permute-start(bf16[10,32,256]{2,1,0:T(8,128)(2,1)S(1)} %get-tuple-element.28), channel_id=1, source_target_pairs={{0,16},{16,0},{1,17},{17,1},{2,18},{18,2},{3,19},{19,3},{4,20},{20... | collective-permute-start | bytes 491528 | tf_op jit(solution)/shard_map/ppermute | solution.py:827
  86.3 1.7 %merge.1 = (f32[8,16,128]{2,1,0:T(8,128)}, f32[2,2,32,128]{3,2,1,0:T(8,128)}) custom-call(f32[8,16,128]{2,1,0:T(8,128)} %get-tuple-element.24.scaled_ref, f32[2,16,128]{2,1,0:T(8,128)} %get-tuple-element.25.own_ref, f32[2,16,128]{2,1,0:T(8,128)} %copy-done.2), custom_call_target="tpu_custom_call" | custom-call | tf_op jit(solution)/shard_map/merge/pallas_call | solution.py:195
  87.9 0.0 collective-permute-done.13.peer_ref
  87.9 0.0 collective-permute-done.10
  87.9 2.9 %combine.4.refs_0_ = f32[8,40,32,256]{3,2,1,0:T(8,128)} custom-call(s32[16]{0:T(128)S(1)} %get-tuple-element.18.lookup, f32[2,2,32,128]{3,2,1,0:T(8,128)} %get-tuple-element.26.parts_ref, f32[40,32,256]{2,1,0:T(8,128)S(1)} %get-tuple-element.27.mean_ref, bf16[10,32,256]{2,1,0:T(8,128)(2,1)S(1)} %collective-permute-done.13.peer_ref, ...), custom_call_target="tpu_custom_call" | custom-call | tf_op jit(solution)/shard_map/combine/pallas_call | solution.py:269
  90.9 0.4 collective-permute-done.12.peer_ref
  91.2 2.9 %combine.5.refs_0_ = f32[8,40,32,256]{3,2,1,0:T(8,128)} custom-call(s32[16]{0:T(128)S(1)} %get-tuple-element.18.lookup, f32[2,2,32,128]{3,2,1,0:T(8,128)} %get-tuple-element.26.parts_ref, f32[40,32,256]{2,1,0:T(8,128)S(1)} %get-tuple-element.27.mean_ref, bf16[10,32,256]{2,1,0:T(8,128)(2,1)S(1)} %collective-permute-done.12.peer_ref, ...), custom_call_target="tpu_custom_call", output_to_operand_aliasing={{}: (6, {})} | custom-call | tf_op jit(solution)/shard_map/combine/pallas_call | solution.py:269
  94.1 0.6 collective-permute-done.11.peer_ref
  94.7 2.9 %combine.6.refs_0_ = f32[8,40,32,256]{3,2,1,0:T(8,128)} custom-call(s32[16]{0:T(128)S(1)} %get-tuple-element.18.lookup, f32[2,2,32,128]{3,2,1,0:T(8,128)} %get-tuple-element.26.parts_ref, f32[40,32,256]{2,1,0:T(8,128)S(1)} %get-tuple-element.27.mean_ref, bf16[10,32,256]{2,1,0:T(8,128)(2,1)S(1)} %collective-permute-done.11.peer_ref, ...), custom_call_target="tpu_custom_call", output_to_operand_aliasing={{}: (6, {})} | custom-call | tf_op jit(solution)/shard_map/combine/pallas_call | solution.py:269
  97.6 0.0 collective-permute-done.9.peer_ref
  97.7 2.9 %combine.7 = f32[8,40,32,256]{3,2,1,0:T(8,128)} custom-call(s32[16]{0:T(128)S(1)} %get-tuple-element.18.lookup, f32[2,2,32,128]{3,2,1,0:T(8,128)} %get-tuple-element.26.parts_ref, f32[40,32,256]{2,1,0:T(8,128)S(1)} %get-tuple-element.27.mean_ref, bf16[10,32,256]{2,1,0:T(8,128)(2,1)S(1)} %collective-permute-done.9.peer_ref, ...), custom_call_target="tpu_custom_call", output_to_operand_aliasing={{}: (6, {})} | custom-call | tf_op jit(solution)/shard_map/combine/pallas_call | solution.py:269
  (17 shorter events, 0.0 us)
Async XLA Ops:
  0.7 0.7 copy-start.1
  22.9 14.9 %copy-start.4 = (f32[16]{0:T(128)S(1)}, f32[16]{0:T(128)}, u32[]{:S(2)}) copy-start(f32[16]{0:T(128)} %param.16) | copy-start | bytes 196
  22.9 14.9 %copy-start.5 = (f32[16]{0:T(128)S(1)}, f32[16]{0:T(128)}, u32[]{:S(2)}) copy-start(f32[16]{0:T(128)} %param.22) | copy-start | bytes 196
  22.9 14.9 %copy-start.6 = (f32[64]{0:T(128)S(1)}, f32[64]{0:T(128)}, u32[]{:S(2)}) copy-start(f32[64]{0:T(128)} %param.20) | copy-start | bytes 772
  22.9 14.9 %copy-start.7 = (f32[64]{0:T(128)S(1)}, f32[64]{0:T(128)}, u32[]{:S(2)}) copy-start(f32[64]{0:T(128)} %param.18) | copy-start | bytes 772
  22.9 65.0 %collective-permute-start.10 = (bf16[1,4,40,32,256]{4,3,2,1,0:T(8,128)(2,1)}, bf16[1,4,40,32,256]{4,3,2,1,0:T(8,128)(2,1)}, u32[]{:S(2)}, u32[]{:S(2)}) collective-permute-start(bf16[1,4,40,32,256]{4,3,2,1,0:T(8,128)(2,1)} %get-tuple-element.29), channel_id=1, source_target_pairs={{0,16},{16,0},{1,17},{17,1},{2,18},{18,2},{3,19},{19,3},{4,20},{20... | collective-permute-start | bytes 7864328 | tf_op jit(solution)/shard_map/ppermute | solution.py:804
  26.0 4.4 %collective-permute-start = (bf16[8,64,128]{2,1,0:T(8,128)(2,1)S(1)}, bf16[8,64,128]{2,1,0:T(8,128)(2,1)S(1)}, u32[]{:S(2)}, u32[]{:S(2)}) collective-permute-start(bf16[8,64,128]{2,1,0:T(8,128)(2,1)S(1)} %get-tuple-element.20.own_e.refs_2_), channel_id=1, source_target_pairs={{0,1},{1,2},{2,3},{3,0},{4,5},{5,6},{6,7},{7,4},{8,9},{9,10},{10,1... | collective-permute-start | bytes 393224 | tf_op jit(solution)/shard_map/ppermute | solution.py:753
  26.0 4.8 %collective-permute-start.1 = (bf16[8,64,128]{2,1,0:T(8,128)(2,1)S(1)}, bf16[8,64,128]{2,1,0:T(8,128)(2,1)S(1)}, u32[]{:S(2)}, u32[]{:S(2)}) collective-permute-start(bf16[8,64,128]{2,1,0:T(8,128)(2,1)S(1)} %get-tuple-element.21.own_w.refs_3_), channel_id=1, source_target_pairs={{1,0},{2,1},{3,2},{0,3},{5,4},{6,5},{7,6},{4,7},{9,8},{10,9},{11,1... | collective-permute-start | bytes 393224 | tf_op jit(solution)/shard_map/ppermute | solution.py:754
  33.0 18.1 %collective-permute-start.2 = (bf16[26,64,128]{2,1,0:T(8,128)(2,1)S(1)}, bf16[26,64,128]{2,1,0:T(8,128)(2,1)S(1)}, u32[]{:S(2)}, u32[]{:S(2)}) collective-permute-start(bf16[26,64,128]{2,1,0:T(8,128)(2,1)S(1)} %get-tuple-element.22), channel_id=1, source_target_pairs={{0,4},{4,8},{8,12},{1,5},{5,9},{9,13},{2,6},{6,10},{10,14},{3,7},{... | collective-permute-start | bytes 1277960 | tf_op jit(solution)/shard_map/ppermute | solution.py:758
  36.5 14.6 %collective-permute-start.3 = (bf16[26,64,128]{2,1,0:T(8,128)(2,1)S(1)}, bf16[26,64,128]{2,1,0:T(8,128)(2,1)S(1)}, u32[]{:S(2)}, u32[]{:S(2)}) collective-permute-start(bf16[26,64,128]{2,1,0:T(8,128)(2,1)S(1)} %get-tuple-element.23), channel_id=1, source_target_pairs={{4,0},{8,4},{12,8},{5,1},{9,5},{13,9},{6,2},{10,6},{14,10},{7,3},{... | collective-permute-start | bytes 1277960 | tf_op jit(solution)/shard_map/ppermute | solution.py:759
  38.6 30.9 %copy-start.3 = (f32[16,48,1]{1,0,2:T(8,128)S(1)}, f32[16,48,1]{1,0,2:T(8,128)}, u32[]{:S(2)}) copy-start(f32[16,48,1]{1,0,2:T(8,128)} %constant.33) | copy-start | bytes 9220
  38.6 35.9 %slice-start = ((s8[5242880]{0:T(1024)(128)(4,1)}), s8[4194304]{0:T(1024)(128)(4,1)S(1)}, s32[]{:S(2)}) async-start(s8[5242880]{0:T(1024)(128)(4,1)} %bitcast.23), calls=%async_computation | async-start | bytes 8388608
  51.1 23.5 %slice-start.1 = ((s8[5242880]{0:T(1024)(128)(4,1)}), s8[1048576]{0:T(1024)(128)(4,1)S(1)}, s32[]{:S(2)}) async-start(s8[5242880]{0:T(1024)(128)(4,1)} %bitcast.23), calls=%async_computation.1 | async-start | bytes 2097152
  51.1 23.4 %copy-start = (f32[384,128]{1,0:T(8,128)S(1)}, f32[384,128]{1,0:T(8,128)}, u32[]{:S(2)}) copy-start(f32[384,128]{1,0:T(8,128)} %constant.27.clone.band_ref) | copy-start | bytes 589828
  60.6 7.2 %collective-permute-start.5 = (f32[8,16,128]{2,1,0:T(8,128)S(1)}, f32[8,16,128]{2,1,0:T(8,128)S(1)}, u32[]{:S(2)}, u32[]{:S(2)}) collective-permute-start(f32[8,16,128]{2,1,0:T(8,128)S(1)} %outer_misfits.1), channel_id=1, source_target_pairs={{4,0},{8,4},{12,8},{5,1},{9,5},{13,9},{6,2},{10,6},{14,10},{7,3},{... | collective-permute-start | bytes 196616 | tf_op jit(solution)/shard_map/ppermute | solution.py:28
  61.9 7.6 %collective-permute-start.4 = (f32[8,16,128]{2,1,0:T(8,128)S(1)}, f32[8,16,128]{2,1,0:T(8,128)S(1)}, u32[]{:S(2)}, u32[]{:S(2)}) collective-permute-start(f32[8,16,128]{2,1,0:T(8,128)S(1)} %outer_misfits.1), channel_id=1, source_target_pairs={{0,4},{4,8},{8,12},{1,5},{5,9},{9,13},{2,6},{6,10},{10,14},{3,7},{... | collective-permute-start | bytes 196616 | tf_op jit(solution)/shard_map/ppermute | solution.py:27
  69.7 2.3 %collective-permute-start.7 = (f32[8,16,128]{2,1,0:T(8,128)S(1)}, f32[8,16,128]{2,1,0:T(8,128)S(1)}, u32[]{:S(2)}, u32[]{:S(2)}) collective-permute-start(f32[8,16,128]{2,1,0:T(8,128)S(1)} %convolution_bitcast_fusion.own_ref), channel_id=1, source_target_pairs={{1,0},{2,1},{3,2},{0,3},{5,4},{6,5},{7,6},{4,7},{9,8},{10,9},{11,1... | collective-permute-start | bytes 196616 | tf_op jit(solution)/shard_map/ppermute | solution.py:817
  70.2 4.4 %collective-permute-start.6 = (f32[8,16,128]{2,1,0:T(8,128)S(1)}, f32[8,16,128]{2,1,0:T(8,128)S(1)}, u32[]{:S(2)}, u32[]{:S(2)}) collective-permute-start(f32[8,16,128]{2,1,0:T(8,128)S(1)} %convolution_bitcast_fusion.own_ref), channel_id=1, source_target_pairs={{0,1},{1,2},{2,3},{3,0},{4,5},{5,6},{6,7},{7,4},{8,9},{9,10},{10,1... | collective-permute-start | bytes 196616 | tf_op jit(solution)/shard_map/ppermute | solution.py:816
  78.2 6.0 %collective-permute-start.8 = (f32[2,16,128]{2,1,0:T(8,128)}, f32[2,16,128]{2,1,0:T(8,128)S(1)}, u32[]{:S(2)}, u32[]{:S(2)}) collective-permute-start(f32[2,16,128]{2,1,0:T(8,128)} %get-tuple-element.25.own_ref), channel_id=1, source_target_pairs={{0,16},{16,0},{1,17},{17,1},{2,18},{18,2},{3,19},{19,3},{4,20},{20... | collective-permute-start | bytes 49160 | tf_op jit(solution)/shard_map/ppermute | solution.py:826
  78.8 9.2 %collective-permute-start.13 = (bf16[10,32,256]{2,1,0:T(8,128)(2,1)S(1)}, bf16[10,32,256]{2,1,0:T(8,128)(2,1)S(1)}, u32[]{:S(2)}, u32[]{:S(2)}) collective-permute-start(bf16[10,32,256]{2,1,0:T(8,128)(2,1)S(1)} %get-tuple-element.32), channel_id=1, source_target_pairs={{0,16},{16,0},{1,17},{17,1},{2,18},{18,2},{3,19},{19,3},{4,20},{20... | collective-permute-start | bytes 491528 | tf_op jit(solution)/shard_map/ppermute | solution.py:827
  80.2 11.0 %collective-permute-start.12 = (bf16[10,32,256]{2,1,0:T(8,128)(2,1)S(1)}, bf16[10,32,256]{2,1,0:T(8,128)(2,1)S(1)}, u32[]{:S(2)}, u32[]{:S(2)}) collective-permute-start(bf16[10,32,256]{2,1,0:T(8,128)(2,1)S(1)} %get-tuple-element.31), channel_id=1, source_target_pairs={{0,16},{16,0},{1,17},{17,1},{2,18},{18,2},{3,19},{19,3},{4,20},{20... | collective-permute-start | bytes 491528 | tf_op jit(solution)/shard_map/ppermute | solution.py:827
  80.8 14.0 %collective-permute-start.11 = (bf16[10,32,256]{2,1,0:T(8,128)(2,1)S(1)}, bf16[10,32,256]{2,1,0:T(8,128)(2,1)S(1)}, u32[]{:S(2)}, u32[]{:S(2)}) collective-permute-start(bf16[10,32,256]{2,1,0:T(8,128)(2,1)S(1)} %get-tuple-element.30), channel_id=1, source_target_pairs={{0,16},{16,0},{1,17},{17,1},{2,18},{18,2},{3,19},{19,3},{4,20},{20... | collective-permute-start | bytes 491528 | tf_op jit(solution)/shard_map/ppermute | solution.py:827
  84.2 2.1 %copy-start.2 = (f32[2,16,128]{2,1,0:T(8,128)}, f32[2,16,128]{2,1,0:T(8,128)S(1)}, u32[]{:S(2)}) copy-start(f32[2,16,128]{2,1,0:T(8,128)S(1)} %collective-permute-done.8.other_ref) | copy-start | bytes 49156
  84.2 13.4 %collective-permute-start.9 = (bf16[10,32,256]{2,1,0:T(8,128)(2,1)S(1)}, bf16[10,32,256]{2,1,0:T(8,128)(2,1)S(1)}, u32[]{:S(2)}, u32[]{:S(2)}) collective-permute-start(bf16[10,32,256]{2,1,0:T(8,128)(2,1)S(1)} %get-tuple-element.28), channel_id=1, source_target_pairs={{0,16},{16,0},{1,17},{17,1},{2,18},{18,2},{3,19},{19,3},{4,20},{20... | collective-permute-start | bytes 491528 | tf_op jit(solution)/shard_map/ppermute | solution.py:827

commit v2 on v1

--- a/solution.py
+++ b/solution.py
@@ -295,7 +295,9 @@
 PACKED = 4
 
 
-def entry_layer(ancestors, place, prior_states, weights, targets, seats):
+def entry_layer(ancestors, place, prior_states, weights, targets, seats, span, earlier):
+    begin, steps = span[0], span[1] - span[0]
+    picking = earlier is None
     members, heights, rows, cols = prior_states.shape
     tiles = tiles_of(rows, cols)
     count = len(tiles)
@@ -305,9 +307,15 @@
     pixel_rows, pixel_cols = rows // 2, cols // 2
 
     def kernel(
-        ancestor, spot, prior, weight, field, out, east_ref, west_ref, picked, table,
-        sorted_cells, lines, even_ref, odd_ref, east, west, buffer, used, seen, sems,
+        ancestor, spot, prior, *refs
     ):
+        if picking:
+            weight, field, out, east_ref, west_ref, picked, table, even_ref, odd_ref = refs[:9]
+            sorted_cells, lines, east, west, buffer, used, seen, sems = refs[9:]
+        else:
+            even_ref, odd_ref = refs[:2]
+            out, east_ref, west_ref, sorted_cells, lines, east, west = refs[5:]
+
         def transfer(target, seat, member, tile, leaving):
             window = tile_window(*tiles[tile])
             here = buffer.at[(target, seat, slice(None)) + window]
@@ -330,8 +338,7 @@
             transfer(target, seat, 0, tile, False).wait()
             transfer(target, seat, 0, tile, True).start()
 
-        @pl.when(pl.program_id(0) == 0)
-        def _():
+        def note_parents():
             own = spot[0]
             for target in range(targets):
                 for tile in range(count):
@@ -359,23 +366,25 @@
                     table[slot * count + tile] = jnp.where(
                         group == own, parent - own * members, members + line
                     )
+        @pl.when(pl.program_id(0) == 0)
+        def _():
+            if picking:
+                note_parents()
+                even_ref[...] = jnp.zeros_like(even_ref)
+                odd_ref[...] = jnp.zeros_like(odd_ref)
+                for down in range(5):
+                    for along in range(5):
+                        part = weight[down, along].astype(jnp.float32).T.astype(jnp.bfloat16)
+                        taps = odd_ref if along % 2 else even_ref
+                        line = along // 2 * channels
+                        taps[line : line + channels, down * padded : down * padded + heights] = part
             lines[...] = jnp.zeros_like(lines)
-            even_ref[...] = jnp.zeros_like(even_ref)
-            odd_ref[...] = jnp.zeros_like(odd_ref)
-            for down in range(5):
-                for along in range(5):
-                    part = weight[down, along].astype(jnp.float32).T.astype(jnp.bfloat16)
-                    taps = odd_ref if along % 2 else even_ref
-                    line = along // 2 * channels
-                    taps[line : line + channels, down * padded : down * padded + heights] = part
-
-        @pl.when(pl.program_id(0) == members // 2)
-        def _():
-            each_seat(load_then_send)
-
-        @pl.when(pl.program_id(0) == members - 1)
-        def _():
-            each_seat(lambda target, seat, tile: transfer(target, seat, 0, tile, True).wait())
+
+        if picking:
+
+            @pl.when(pl.program_id(0) == steps // 2)
+            def _():
+                each_seat(load_then_send)
 
         here = lax.broadcasted_iota(jnp.int32, (cols, cols), 0)
         there = lax.broadcasted_iota(jnp.int32, (cols, cols), 1)
@@ -428,51 +437,72 @@
                 west[...] = jnp.where((lane >= 64 + at) & (lane < 67 + at), onward, west[...])
         east_ref[0] = east[...].astype(jnp.bfloat16)
         west_ref[0] = west[...].astype(jnp.bfloat16)
+        if picking:
+
+            @pl.when(pl.program_id(0) == steps - 1)
+            def _():
+                each_seat(lambda target, seat, tile: transfer(target, seat, 0, tile, True).wait())
 
     sent = (targets, seats, heights, rows, cols)
+    picked_shapes = (
+        pltpu.HBM(sent, prior_states.dtype),
+        jax.ShapeDtypeStruct((members * count,), jnp.int32),
+        jax.ShapeDtypeStruct((3 * channels, 5 * padded), prior_states.dtype),
+        jax.ShapeDtypeStruct((2 * channels, 5 * padded), prior_states.dtype),
+    )
+    tap_specs = [
+        pl.BlockSpec((size * channels, 5 * padded), lambda i: (0, 0)) for size in (3, 2)
+    ]
     edge = jax.ShapeDtypeStruct((members, channels, pixel_cols), jnp.bfloat16)
-    edge_spec = pl.BlockSpec((1, channels, pixel_cols), lambda i: (i, 0, 0))
+    edge_spec = pl.BlockSpec((1, channels, pixel_cols), lambda i: (begin + i, 0, 0))
     return pl.pallas_call(
         kernel,
-        grid=(members,),
+        grid=(steps,),
         out_shape=(
             pltpu.HBM((members, pixel_rows + 2, channels, pixel_cols), jnp.float32),
             edge,
             edge,
-            pltpu.HBM(sent, prior_states.dtype),
-            jax.ShapeDtypeStruct((members * count,), jnp.int32),
-        ),
+        )
+        + picked_shapes * picking,
         in_specs=[
             pl.BlockSpec(memory_space=pltpu.SMEM),
             pl.BlockSpec(memory_space=pltpu.SMEM),
-            pl.BlockSpec((1, heights, rows, cols), lambda i: (i, 0, 0, 0)),
-            pl.BlockSpec(weights.shape, lambda i: (0, 0, 0, 0)),
-            pl.BlockSpec(memory_space=pltpu.HBM),
-        ],
+            pl.BlockSpec((1, heights, rows, cols), lambda i: (begin + i, 0, 0, 0)),
+        ]
+        + (
+            [
+                pl.BlockSpec(weights.shape, lambda i: (0, 0, 0, 0)),
+                pl.BlockSpec(memory_space=pltpu.HBM),
+            ]
+            if picking
+            else tap_specs + [pl.BlockSpec(memory_space=pltpu.HBM)] * 3
+        ),
         out_specs=(
-            pl.BlockSpec((1, pixel_rows + 2, channels, pixel_cols), lambda i: (i, 0, 0, 0)),
+            pl.BlockSpec((1, pixel_rows + 2, channels, pixel_cols), lambda i: (begin + i, 0, 0, 0)),
             edge_spec,
             edge_spec,
-            pl.BlockSpec(memory_space=pltpu.HBM),
-            pl.BlockSpec(memory_space=pltpu.SMEM),
-        ),
+        )
+        + (pl.BlockSpec(memory_space=pltpu.HBM), pl.BlockSpec(memory_space=pltpu.SMEM), *tap_specs)
+        * picking,
+        input_output_aliases={} if picking else {5: 0, 6: 1, 7: 2},
         scratch_shapes=[
             pltpu.VMEM((2, heights * rows, pixel_cols), jnp.float32),
             pltpu.VMEM((2, rows + 8, padded, pixel_cols), jnp.bfloat16),
-            pltpu.VMEM((3 * channels, 5 * padded), jnp.bfloat16),
-            pltpu.VMEM((2 * channels, 5 * padded), jnp.bfloat16),
             pltpu.VMEM((channels, pixel_cols), jnp.float32),
             pltpu.VMEM((channels, pixel_cols), jnp.float32),
+        ]
+        + [
             pltpu.VMEM(sent, prior_states.dtype),
             pltpu.SMEM((targets * count,), jnp.int32),
             pltpu.SMEM((groups,), jnp.int32),
             pltpu.SemaphoreType.DMA((2, targets, seats, count)),
-        ],
+        ]
+        * picking,
         compiler_params=pltpu.CompilerParams(
             vmem_limit_bytes=(12 << 20) + 2 * math.prod(sent)
         ),
         name="entry_layer",
-    )(ancestors, place, prior_states, weights, prior_states)
+    )(ancestors, place, prior_states, *(earlier or (weights, prior_states)))
 
 
 def received_sides(from_west, from_east, border):
@@ -740,14 +770,12 @@
     borders = jnp.stack(
         [lat, lax.axis_size("lat") - 1 - lat, lon, lax.axis_size("lon") - 1 - lon]
     ).astype(jnp.int32)
-    partial, own_east, own_west, picked, table = entry_layer(
-        ancestors,
-        place,
-        held(prior_states),
-        held(jnp.transpose(entry_layer_stencil, (2, 3, 1, 0))),
-        targets,
-        seats,
-    )
+    members = prior_states.shape[0]
+    weights = held(jnp.transpose(entry_layer_stencil, (2, 3, 1, 0)))
+    common = (ancestors, place, held(prior_states), weights, targets, seats)
+    first = max(1, 3 * members // 8)
+    *ends, picked, table, even, odd = entry_layer(*common, (0, first), None)
+    partial, own_east, own_west = entry_layer(*common, (first, members), (even, odd, *ends))
     count = lax.axis_size("lon")
     ring = [(i, (i + 1) % count) for i in range(count)]
     from_west = lax.ppermute(own_east, "lon", ring)

time: 101 us -> 101 us (level)
  Pallas kernels: 62.6 us -> 64.3 us
  starting transfers between devices: 22.7 us -> 21.1 us
    ppermute x1, waiting for transfers between devices: 1.93 us -> 0.04 us  [body(): other_norm = lax.ppermute(own_norm, 'ens', swap)]
    pallas_call x1 -> x2, Pallas kernels: 21.5 us -> 23.2 us  [entry_layer(): pl.pallas_call(kernel, grid=(steps,), out_shape=(pltpu.HBM((members, pixe...]
    ppermute x4, starting transfers between devices: 5.57 us -> 4.01 us  [body(): others = [lax.ppermute(piece, 'ens', swap) for piece in sent]]
    ppermute x4, waiting for transfers between devices: 0.99 us -> 2.49 us  [body(): others = [lax.ppermute(piece, 'ens', swap) for piece in sent]]
  transfers between devices with their start and end apart: 14 -> 14, of which waited for: 9 -> 9; matrix products, arithmetic and copies ran while one was open for 1% -> 1% of each run, Pallas kernels for 38% -> 51%
where the time goes in v2:
time: 101 us; the launch traced here: 100 us
  Pallas kernels  64.3 us (64%)
  starting transfers between devices  21.1 us (21%)
  waiting for transfers between devices  12.2 us (12%)
  local copies, waits for them, and re-layouts  1.55 us (2%)
    pallas_call x2, Pallas kernels, entry_layer(): pl.pallas_call(kernel, grid=(steps,), out_shape=(pltpu.HBM((members, pixe...  23.2 us
    pallas_call x2, Pallas kernels, misfits(): pl.pallas_call(kernel, grid=(members,), out_shape=jax.ShapeDtypeStruct((m...  22 us
    pallas_call x4, Pallas kernels, combine(): pl.pallas_call(kernel, grid=(steps,), out_shape=jax.ShapeDtypeStruct(prio...  11.6 us
    ppermute x1, starting transfers between devices, extended(): before = lax.ppermute(last, axis, up)  5.17 us
    ppermute x4, starting transfers between devices, body(): others = [lax.ppermute(piece, 'ens', swap) for piece in sent]  4.01 us
    pallas_call x1, Pallas kernels, group_mean(): pl.pallas_call(kernel, grid=(heights // chunk,), out_shape=(pltpu.HBM(smo...  3.66 us
    ppermute x1, starting transfers between devices, departures(): from_north = lax.ppermute(south, 'lat', onward)  3.48 us
    ppermute x1, starting transfers between devices, body(): received = lax.ppermute(picked, 'ens', swap)  3 us
  transfers between devices with their start and end apart: 14, of which 9 were waited for; matrix products, arithmetic and copies ran while one was open for 1% of the time, Pallas kernels for 51%

profile of v2, /device:TPU:0, one launch (start us, length us, event | category | flops | bytes accessed | tf_op | source)
XLA Modules:
  0.0 100.4 jit_solution(12716789391517731693)
XLA Ops:
  0.6 0.1 pad_add_fusion.spot
  0.7 0.7 copy-done.1
  1.4 9.8 %entry_layer.2 = (f32[8,18,64,128]{3,2,1,0:T(8,128)}, bf16[8,64,128]{2,1,0:T(8,128)(2,1)S(1)}, bf16[8,64,128]{2,1,0:T(8,128)(2,1)S(1)}, bf16[1,4,40,32,256]{4,3,...) custom-call(s32[2,16]{1,0:T(2,128)S(1)} %bitcast.25, ...), custom_call_target="tpu_custom_call" | custom-call | tf_op jit(solution)/shard_map/entry_layer/pallas_call | solution.py:458
  11.2 3.0 %collective-permute-start.10 = (bf16[1,4,40,32,256]{4,3,2,1,0:T(8,128)(2,1)}, bf16[1,4,40,32,256]{4,3,2,1,0:T(8,128)(2,1)}, u32[]{:S(2)}, u32[]{:S(2)}) collective-permute-start(bf16[1,4,40,32,256]{4,3,2,1,0:T(8,128)(2,1)} %get-tuple-element.39), channel_id=1, source_target_pairs={{0,16},{16,0},{1,17},{17,1},{2,18},{18,2},{3,19},{19,3},{4,20},{20... | collective-permute-start | bytes 7864328 | tf_op jit(solution)/shard_map/ppermute | solution.py:832
  14.2 13.5 %entry_layer.3 = (f32[8,18,64,128]{3,2,1,0:T(8,128)}, bf16[8,64,128]{2,1,0:T(8,128)(2,1)S(1)}, bf16[8,64,128]{2,1,0:T(8,128)(2,1)S(1)}) custom-call(s32[2,16]{1,0:T(2,128)S(1)} %bitcast.26, s32[2]{0:T(128)S(1)} %pad_add_fusion.spot, bf16[8,40,32,256]{3,2,1,0:T(8,128)(2,1)} %prior.13, ...), custom_call_target="tpu_custom_call", output_to_operand_aliasing={{0}: (5, {}), {1}: (6, {}), {2}: (7, {})} | custom-call | tf_op jit(solution)/shard_map/entry_layer/pallas_call | solution.py:458
  27.7 0.0 copy-start.7
  27.7 0.1 collective-permute-start
  27.7 1.7 %collective-permute-start.1 = (bf16[8,64,128]{2,1,0:T(8,128)(2,1)S(1)}, bf16[8,64,128]{2,1,0:T(8,128)(2,1)S(1)}, u32[]{:S(2)}, u32[]{:S(2)}) collective-permute-start(bf16[8,64,128]{2,1,0:T(8,128)(2,1)S(1)} %get-tuple-element.31.own_w.refs_3_), channel_id=1, source_target_pairs={{1,0},{2,1},{3,2},{0,3},{5,4},{6,5},{7,6},{4,7},{9,8},{10,9},{11,1... | collective-permute-start | bytes 393224 | tf_op jit(solution)/shard_map/ppermute | solution.py:782
  29.5 0.1 pad_add_fusion.1.border.refs_0_
  29.5 2.6 %collective-permute-done.left.refs_4_ = bf16[8,64,128]{2,1,0:T(8,128)(2,1)S(1)} collective-permute-done((bf16[8,64,128]{2,1,0:T(8,128)(2,1)S(1)}, bf16[8,64,128]{2,1,0:T(8,128)(2,1)S(1)}, u32[]{:S(2)}, u32[]{:S(2)}) %collective-permute-start) | collective-permute-done | bytes 131104 | tf_op jit(solution)/shard_map/ppermute | solution.py:781
  32.1 0.5 collective-permute-done.1.right.refs_5_
  32.6 2.2 %row_ends.1 = (bf16[26,64,128]{2,1,0:T(8,128)(2,1)S(1)}, bf16[26,64,128]{2,1,0:T(8,128)(2,1)S(1)}) custom-call(s32[4]{0:T(128)S(1)} %pad_add_fusion.1.border.refs_0_, f32[8,18,64,128]{3,2,1,0:T(8,128)} %get-tuple-element.29.top.bottom.refs_1_, f32[8,18,64,128]{3,2,1,0:T(8,128)} %get-tuple-element.29.top.bottom.refs_1_, ...), custom_call_target="tpu_custom_call" | custom-call | tf_op jit(solution)/shard_map/row_ends/pallas_call | solution.py:562
  34.8 3.5 %collective-permute-start.2 = (bf16[26,64,128]{2,1,0:T(8,128)(2,1)S(1)}, bf16[26,64,128]{2,1,0:T(8,128)(2,1)S(1)}, u32[]{:S(2)}, u32[]{:S(2)}) collective-permute-start(bf16[26,64,128]{2,1,0:T(8,128)(2,1)S(1)} %get-tuple-element.32), channel_id=1, source_target_pairs={{0,4},{4,8},{8,12},{1,5},{5,9},{9,13},{2,6},{6,10},{10,14},{3,7},{... | collective-permute-start | bytes 1277960 | tf_op jit(solution)/shard_map/ppermute | solution.py:786
  38.3 1.3 %collective-permute-start.3 = (bf16[26,64,128]{2,1,0:T(8,128)(2,1)S(1)}, bf16[26,64,128]{2,1,0:T(8,128)(2,1)S(1)}, u32[]{:S(2)}, u32[]{:S(2)}) collective-permute-start(bf16[26,64,128]{2,1,0:T(8,128)(2,1)S(1)} %get-tuple-element.33), channel_id=1, source_target_pairs={{4,0},{8,4},{12,8},{5,1},{9,5},{13,9},{6,2},{10,6},{14,10},{7,3},{... | collective-permute-start | bytes 1277960 | tf_op jit(solution)/shard_map/ppermute | solution.py:787
  39.7 0.7 copy.25.refs_6_.refs_11_
  40.4 12.5 %inner_misfits.1.refs_10_ = f32[8,16,128]{2,1,0:T(8,128)S(1)} custom-call(s32[4]{0:T(128)S(1)} %pad_add_fusion.1.border.refs_0_, f32[8,18,64,128]{3,2,1,0:T(8,128)} %get-tuple-element.29.top.bottom.refs_1_, bf16[8,64,128]{2,1,0:T(8,128)(2,1)S(1)} %get-tuple-element.30.own_e.refs_2_, bf16[8,64,128]{2,1,0:T(8,128)(2,1)S(1)} %get-tuple-element.31.own_w.refs_3_, ...), custom_call_target="tpu_custom_call" | custom-call | tf_op jit(solution)/shard_map/inner_misfits/pallas_call | solution.py:724
  52.9 0.0 slice-start.1
  52.9 0.0 copy-start
  52.9 0.0 collective-permute-done.2.refs_6_.refs_8_
  52.9 0.0 collective-permute-done.3.refs_7_.refs_9_
  52.9 9.5 %outer_misfits.1 = f32[8,16,128]{2,1,0:T(8,128)S(1)} custom-call(s32[4]{0:T(128)S(1)} %pad_add_fusion.1.border.refs_0_, f32[8,18,64,128]{3,2,1,0:T(8,128)} %get-tuple-element.29.top.bottom.refs_1_, bf16[8,64,128]{2,1,0:T(8,128)(2,1)S(1)} %get-tuple-element.30.own_e.refs_2_, bf16[8,64,128]{2,1,0:T(8,128)(2,1)S(1)} %get-tuple-element.31.own_w.refs_3_, ...), custom_call_target="tpu_custom_call" | custom-call | tf_op jit(solution)/shard_map/outer_misfits/pallas_call | solution.py:724
  62.4 1.3 %collective-permute-start.5 = (f32[8,16,128]{2,1,0:T(8,128)S(1)}, f32[8,16,128]{2,1,0:T(8,128)S(1)}, u32[]{:S(2)}, u32[]{:S(2)}) collective-permute-start(f32[8,16,128]{2,1,0:T(8,128)S(1)} %outer_misfits.1), channel_id=1, source_target_pairs={{4,0},{8,4},{12,8},{5,1},{9,5},{13,9},{6,2},{10,6},{14,10},{7,3},{... | collective-permute-start | bytes 196616 | tf_op jit(solution)/shard_map/ppermute | solution.py:28
  63.7 5.2 %collective-permute-start.4 = (f32[8,16,128]{2,1,0:T(8,128)S(1)}, f32[8,16,128]{2,1,0:T(8,128)S(1)}, u32[]{:S(2)}, u32[]{:S(2)}) collective-permute-start(f32[8,16,128]{2,1,0:T(8,128)S(1)} %outer_misfits.1), channel_id=1, source_target_pairs={{0,4},{4,8},{8,12},{1,5},{5,9},{9,13},{2,6},{6,10},{10,14},{3,7},{... | collective-permute-start | bytes 196616 | tf_op jit(solution)/shard_map/ppermute | solution.py:27
  68.9 0.7 collective-permute-done.5
  69.5 1.7 %collective-permute-done.4 = f32[8,16,128]{2,1,0:T(8,128)S(1)} collective-permute-done((f32[8,16,128]{2,1,0:T(8,128)S(1)}, f32[8,16,128]{2,1,0:T(8,128)S(1)}, u32[]{:S(2)}, u32[]{:S(2)}) %collective-permute-start.4) | collective-permute-done | bytes 65568 | tf_op jit(solution)/shard_map/ppermute | solution.py:27
  71.3 0.2 convolution_bitcast_fusion.own_ref
  71.5 0.4 collective-permute-start.7
  71.9 0.1 collective-permute-start.6
  72.1 1.8 %collective-permute-done.7.right = f32[8,16,128]{2,1,0:T(8,128)S(1)} collective-permute-done((f32[8,16,128]{2,1,0:T(8,128)S(1)}, f32[8,16,128]{2,1,0:T(8,128)S(1)}, u32[]{:S(2)}, u32[]{:S(2)}) %collective-permute-start.7) | collective-permute-done | bytes 65568 | tf_op jit(solution)/shard_map/ppermute | solution.py:845
  73.8 2.4 %collective-permute-done.6.left = f32[8,16,128]{2,1,0:T(8,128)S(1)} collective-permute-done((f32[8,16,128]{2,1,0:T(8,128)S(1)}, f32[8,16,128]{2,1,0:T(8,128)S(1)}, u32[]{:S(2)}, u32[]{:S(2)}) %collective-permute-start.6) | collective-permute-done | bytes 65568 | tf_op jit(solution)/shard_map/ppermute | solution.py:844
  76.3 3.7 %group_mean.1 = (f32[8,16,128]{2,1,0:T(8,128)}, f32[2,16,128]{2,1,0:T(8,128)}, f32[40,32,256]{2,1,0:T(8,128)S(1)}, bf16[10,32,256]{2,1,0:T(8,128)(2,1)S(1)}, bf1...) custom-call(s32[4]{0:T(128)S(1)} %pad_add_fusion.1.border.refs_0_, ...), custom_call_target="tpu_custom_call" | custom-call | tf_op jit(solution)/shard_map/group_mean/pallas_call | solution.py:147
  80.0 0.5 collective-permute-start.8
  80.5 1.5 %collective-permute-start.13 = (bf16[10,32,256]{2,1,0:T(8,128)(2,1)S(1)}, bf16[10,32,256]{2,1,0:T(8,128)(2,1)S(1)}, u32[]{:S(2)}, u32[]{:S(2)}) collective-permute-start(bf16[10,32,256]{2,1,0:T(8,128)(2,1)S(1)} %get-tuple-element.42), channel_id=1, source_target_pairs={{0,16},{16,0},{1,17},{17,1},{2,18},{18,2},{3,19},{19,3},{4,20},{20... | collective-permute-start | bytes 491528 | tf_op jit(solution)/shard_map/ppermute | solution.py:855
  82.0 0.5 collective-permute-start.12
  82.5 1.5 %collective-permute-start.11 = (bf16[10,32,256]{2,1,0:T(8,128)(2,1)S(1)}, bf16[10,32,256]{2,1,0:T(8,128)(2,1)S(1)}, u32[]{:S(2)}, u32[]{:S(2)}) collective-permute-start(bf16[10,32,256]{2,1,0:T(8,128)(2,1)S(1)} %get-tuple-element.40), channel_id=1, source_target_pairs={{0,16},{16,0},{1,17},{17,1},{2,18},{18,2},{3,19},{19,3},{4,20},{20... | collective-permute-start | bytes 491528 | tf_op jit(solution)/shard_map/ppermute | solution.py:855
  84.0 0.0 collective-permute-done.8.other_ref
  84.1 0.5 collective-permute-start.9
  84.6 0.1 copy-done.2
  84.7 1.6 %merge.1 = (f32[8,16,128]{2,1,0:T(8,128)}, f32[2,2,32,128]{3,2,1,0:T(8,128)}) custom-call(f32[8,16,128]{2,1,0:T(8,128)} %get-tuple-element.34.scaled_ref, f32[2,16,128]{2,1,0:T(8,128)} %get-tuple-element.35.own_ref, f32[2,16,128]{2,1,0:T(8,128)} %copy-done.2), custom_call_target="tpu_custom_call" | custom-call | tf_op jit(solution)/shard_map/merge/pallas_call | solution.py:195
  86.3 1.3 %collective-permute-done.13.peer_ref = bf16[10,32,256]{2,1,0:T(8,128)(2,1)S(1)} collective-permute-done((bf16[10,32,256]{2,1,0:T(8,128)(2,1)S(1)}, bf16[10,32,256]{2,1,0:T(8,128)(2,1)S(1)}, u32[]{:S(2)}, u32[]{:S(2)}) %collective-permute-start.13) | collective-permute-done | bytes 163872 | tf_op jit(solution)/shard_map/ppermute | solution.py:855
  87.6 0.0 collective-permute-done.10
  87.6 2.9 %combine.4.refs_0_ = f32[8,40,32,256]{3,2,1,0:T(8,128)} custom-call(s32[16]{0:T(128)S(1)} %get-tuple-element.23.lookup, f32[2,2,32,128]{3,2,1,0:T(8,128)} %get-tuple-element.36.parts_ref, f32[40,32,256]{2,1,0:T(8,128)S(1)} %get-tuple-element.37.mean_ref, bf16[10,32,256]{2,1,0:T(8,128)(2,1)S(1)} %collective-permute-done.13.peer_ref, ...), custom_call_target="tpu_custom_call" | custom-call | tf_op jit(solution)/shard_map/combine/pallas_call | solution.py:269
  90.5 0.6 collective-permute-done.12.peer_ref
  91.1 2.9 %combine.5.refs_0_ = f32[8,40,32,256]{3,2,1,0:T(8,128)} custom-call(s32[16]{0:T(128)S(1)} %get-tuple-element.23.lookup, f32[2,2,32,128]{3,2,1,0:T(8,128)} %get-tuple-element.36.parts_ref, f32[40,32,256]{2,1,0:T(8,128)S(1)} %get-tuple-element.37.mean_ref, bf16[10,32,256]{2,1,0:T(8,128)(2,1)S(1)} %collective-permute-done.12.peer_ref, ...), custom_call_target="tpu_custom_call", output_to_operand_aliasing={{}: (6, {})} | custom-call | tf_op jit(solution)/shard_map/combine/pallas_call | solution.py:269
  94.0 0.6 collective-permute-done.11.peer_ref
  94.6 2.9 %combine.6.refs_0_ = f32[8,40,32,256]{3,2,1,0:T(8,128)} custom-call(s32[16]{0:T(128)S(1)} %get-tuple-element.23.lookup, f32[2,2,32,128]{3,2,1,0:T(8,128)} %get-tuple-element.36.parts_ref, f32[40,32,256]{2,1,0:T(8,128)S(1)} %get-tuple-element.37.mean_ref, bf16[10,32,256]{2,1,0:T(8,128)(2,1)S(1)} %collective-permute-done.11.peer_ref, ...), custom_call_target="tpu_custom_call", output_to_operand_aliasing={{}: (6, {})} | custom-call | tf_op jit(solution)/shard_map/combine/pallas_call | solution.py:269
  97.5 0.0 collective-permute-done.9.peer_ref
  97.5 2.9 %combine.7 = f32[8,40,32,256]{3,2,1,0:T(8,128)} custom-call(s32[16]{0:T(128)S(1)} %get-tuple-element.23.lookup, f32[2,2,32,128]{3,2,1,0:T(8,128)} %get-tuple-element.36.parts_ref, f32[40,32,256]{2,1,0:T(8,128)S(1)} %get-tuple-element.37.mean_ref, bf16[10,32,256]{2,1,0:T(8,128)(2,1)S(1)} %collective-permute-done.9.peer_ref, ...), custom_call_target="tpu_custom_call", output_to_operand_aliasing={{}: (6, {})} | custom-call | tf_op jit(solution)/shard_map/combine/pallas_call | solution.py:269
  (18 shorter events, 0.0 us)
Async XLA Ops:
  0.7 0.7 copy-start.1
  11.2 76.4 %collective-permute-start.10 = (bf16[1,4,40,32,256]{4,3,2,1,0:T(8,128)(2,1)}, bf16[1,4,40,32,256]{4,3,2,1,0:T(8,128)(2,1)}, u32[]{:S(2)}, u32[]{:S(2)}) collective-permute-start(bf16[1,4,40,32,256]{4,3,2,1,0:T(8,128)(2,1)} %get-tuple-element.39), channel_id=1, source_target_pairs={{0,16},{16,0},{1,17},{17,1},{2,18},{18,2},{3,19},{19,3},{4,20},{20... | collective-permute-start | bytes 7864328 | tf_op jit(solution)/shard_map/ppermute | solution.py:832
  27.6 11.9 %copy-start.4 = (f32[16]{0:T(128)S(1)}, f32[16]{0:T(128)}, u32[]{:S(2)}) copy-start(f32[16]{0:T(128)} %param.16) | copy-start | bytes 196
  27.6 12.0 %copy-start.5 = (f32[16]{0:T(128)S(1)}, f32[16]{0:T(128)}, u32[]{:S(2)}) copy-start(f32[16]{0:T(128)} %param.22) | copy-start | bytes 196
  27.6 12.0 %copy-start.6 = (f32[64]{0:T(128)S(1)}, f32[64]{0:T(128)}, u32[]{:S(2)}) copy-start(f32[64]{0:T(128)} %param.20) | copy-start | bytes 772
  27.7 12.0 %copy-start.7 = (f32[64]{0:T(128)S(1)}, f32[64]{0:T(128)}, u32[]{:S(2)}) copy-start(f32[64]{0:T(128)} %param.18) | copy-start | bytes 772
  27.7 4.4 %collective-permute-start = (bf16[8,64,128]{2,1,0:T(8,128)(2,1)S(1)}, bf16[8,64,128]{2,1,0:T(8,128)(2,1)S(1)}, u32[]{:S(2)}, u32[]{:S(2)}) collective-permute-start(bf16[8,64,128]{2,1,0:T(8,128)(2,1)S(1)} %get-tuple-element.30.own_e.refs_2_), channel_id=1, source_target_pairs={{0,1},{1,2},{2,3},{3,0},{4,5},{5,6},{6,7},{7,4},{8,9},{9,10},{10,1... | collective-permute-start | bytes 393224 | tf_op jit(solution)/shard_map/ppermute | solution.py:781
  27.7 4.8 %collective-permute-start.1 = (bf16[8,64,128]{2,1,0:T(8,128)(2,1)S(1)}, bf16[8,64,128]{2,1,0:T(8,128)(2,1)S(1)}, u32[]{:S(2)}, u32[]{:S(2)}) collective-permute-start(bf16[8,64,128]{2,1,0:T(8,128)(2,1)S(1)} %get-tuple-element.31.own_w.refs_3_), channel_id=1, source_target_pairs={{1,0},{2,1},{3,2},{0,3},{5,4},{6,5},{7,6},{4,7},{9,8},{10,9},{11,1... | collective-permute-start | bytes 393224 | tf_op jit(solution)/shard_map/ppermute | solution.py:782
  34.8 18.1 %collective-permute-start.2 = (bf16[26,64,128]{2,1,0:T(8,128)(2,1)S(1)}, bf16[26,64,128]{2,1,0:T(8,128)(2,1)S(1)}, u32[]{:S(2)}, u32[]{:S(2)}) collective-permute-start(bf16[26,64,128]{2,1,0:T(8,128)(2,1)S(1)} %get-tuple-element.32), channel_id=1, source_target_pairs={{0,4},{4,8},{8,12},{1,5},{5,9},{9,13},{2,6},{6,10},{10,14},{3,7},{... | collective-permute-start | bytes 1277960 | tf_op jit(solution)/shard_map/ppermute | solution.py:786
  38.3 14.6 %collective-permute-start.3 = (bf16[26,64,128]{2,1,0:T(8,128)(2,1)S(1)}, bf16[26,64,128]{2,1,0:T(8,128)(2,1)S(1)}, u32[]{:S(2)}, u32[]{:S(2)}) collective-permute-start(bf16[26,64,128]{2,1,0:T(8,128)(2,1)S(1)} %get-tuple-element.33), channel_id=1, source_target_pairs={{4,0},{8,4},{12,8},{5,1},{9,5},{13,9},{6,2},{10,6},{14,10},{7,3},{... | collective-permute-start | bytes 1277960 | tf_op jit(solution)/shard_map/ppermute | solution.py:787
  40.4 30.9 %copy-start.3 = (f32[16,48,1]{1,0,2:T(8,128)S(1)}, f32[16,48,1]{1,0,2:T(8,128)}, u32[]{:S(2)}) copy-start(f32[16,48,1]{1,0,2:T(8,128)} %constant.33) | copy-start | bytes 9220
  40.4 35.9 %slice-start = ((s8[5242880]{0:T(1024)(128)(4,1)}), s8[4194304]{0:T(1024)(128)(4,1)S(1)}, s32[]{:S(2)}) async-start(s8[5242880]{0:T(1024)(128)(4,1)} %bitcast.23), calls=%async_computation | async-start | bytes 8388608
  52.9 23.4 %slice-start.1 = ((s8[5242880]{0:T(1024)(128)(4,1)}), s8[1048576]{0:T(1024)(128)(4,1)S(1)}, s32[]{:S(2)}) async-start(s8[5242880]{0:T(1024)(128)(4,1)} %bitcast.23), calls=%async_computation.1 | async-start | bytes 2097152
  52.9 23.4 %copy-start = (f32[384,128]{1,0:T(8,128)S(1)}, f32[384,128]{1,0:T(8,128)}, u32[]{:S(2)}) copy-start(f32[384,128]{1,0:T(8,128)} %constant.27.clone.band_ref) | copy-start | bytes 589828
  62.4 7.1 %collective-permute-start.5 = (f32[8,16,128]{2,1,0:T(8,128)S(1)}, f32[8,16,128]{2,1,0:T(8,128)S(1)}, u32[]{:S(2)}, u32[]{:S(2)}) collective-permute-start(f32[8,16,128]{2,1,0:T(8,128)S(1)} %outer_misfits.1), channel_id=1, source_target_pairs={{4,0},{8,4},{12,8},{5,1},{9,5},{13,9},{6,2},{10,6},{14,10},{7,3},{... | collective-permute-start | bytes 196616 | tf_op jit(solution)/shard_map/ppermute | solution.py:28
  63.7 7.6 %collective-permute-start.4 = (f32[8,16,128]{2,1,0:T(8,128)S(1)}, f32[8,16,128]{2,1,0:T(8,128)S(1)}, u32[]{:S(2)}, u32[]{:S(2)}) collective-permute-start(f32[8,16,128]{2,1,0:T(8,128)S(1)} %outer_misfits.1), channel_id=1, source_target_pairs={{0,4},{4,8},{8,12},{1,5},{5,9},{9,13},{2,6},{6,10},{10,14},{3,7},{... | collective-permute-start | bytes 196616 | tf_op jit(solution)/shard_map/ppermute | solution.py:27
  71.5 2.3 %collective-permute-start.7 = (f32[8,16,128]{2,1,0:T(8,128)S(1)}, f32[8,16,128]{2,1,0:T(8,128)S(1)}, u32[]{:S(2)}, u32[]{:S(2)}) collective-permute-start(f32[8,16,128]{2,1,0:T(8,128)S(1)} %convolution_bitcast_fusion.own_ref), channel_id=1, source_target_pairs={{1,0},{2,1},{3,2},{0,3},{5,4},{6,5},{7,6},{4,7},{9,8},{10,9},{11,1... | collective-permute-start | bytes 196616 | tf_op jit(solution)/shard_map/ppermute | solution.py:845
  71.9 4.3 %collective-permute-start.6 = (f32[8,16,128]{2,1,0:T(8,128)S(1)}, f32[8,16,128]{2,1,0:T(8,128)S(1)}, u32[]{:S(2)}, u32[]{:S(2)}) collective-permute-start(f32[8,16,128]{2,1,0:T(8,128)S(1)} %convolution_bitcast_fusion.own_ref), channel_id=1, source_target_pairs={{0,1},{1,2},{2,3},{3,0},{4,5},{5,6},{6,7},{7,4},{8,9},{9,10},{10,1... | collective-permute-start | bytes 196616 | tf_op jit(solution)/shard_map/ppermute | solution.py:844
  80.0 4.1 %collective-permute-start.8 = (f32[2,16,128]{2,1,0:T(8,128)}, f32[2,16,128]{2,1,0:T(8,128)S(1)}, u32[]{:S(2)}, u32[]{:S(2)}) collective-permute-start(f32[2,16,128]{2,1,0:T(8,128)} %get-tuple-element.35.own_ref), channel_id=1, source_target_pairs={{0,16},{16,0},{1,17},{17,1},{2,18},{18,2},{3,19},{19,3},{4,20},{20... | collective-permute-start | bytes 49160 | tf_op jit(solution)/shard_map/ppermute | solution.py:854
  80.5 7.1 %collective-permute-start.13 = (bf16[10,32,256]{2,1,0:T(8,128)(2,1)S(1)}, bf16[10,32,256]{2,1,0:T(8,128)(2,1)S(1)}, u32[]{:S(2)}, u32[]{:S(2)}) collective-permute-start(bf16[10,32,256]{2,1,0:T(8,128)(2,1)S(1)} %get-tuple-element.42), channel_id=1, source_target_pairs={{0,16},{16,0},{1,17},{17,1},{2,18},{18,2},{3,19},{19,3},{4,20},{20... | collective-permute-start | bytes 491528 | tf_op jit(solution)/shard_map/ppermute | solution.py:855
  82.0 9.1 %collective-permute-start.12 = (bf16[10,32,256]{2,1,0:T(8,128)(2,1)S(1)}, bf16[10,32,256]{2,1,0:T(8,128)(2,1)S(1)}, u32[]{:S(2)}, u32[]{:S(2)}) collective-permute-start(bf16[10,32,256]{2,1,0:T(8,128)(2,1)S(1)} %get-tuple-element.41), channel_id=1, source_target_pairs={{0,16},{16,0},{1,17},{17,1},{2,18},{18,2},{3,19},{19,3},{4,20},{20... | collective-permute-start | bytes 491528 | tf_op jit(solution)/shard_map/ppermute | solution.py:855
  82.5 12.1 %collective-permute-start.11 = (bf16[10,32,256]{2,1,0:T(8,128)(2,1)S(1)}, bf16[10,32,256]{2,1,0:T(8,128)(2,1)S(1)}, u32[]{:S(2)}, u32[]{:S(2)}) collective-permute-start(bf16[10,32,256]{2,1,0:T(8,128)(2,1)S(1)} %get-tuple-element.40), channel_id=1, source_target_pairs={{0,16},{16,0},{1,17},{17,1},{2,18},{18,2},{3,19},{19,3},{4,20},{20... | collective-permute-start | bytes 491528 | tf_op jit(solution)/shard_map/ppermute | solution.py:855
  84.1 0.6 copy-start.2
  84.1 13.4 %collective-permute-start.9 = (bf16[10,32,256]{2,1,0:T(8,128)(2,1)S(1)}, bf16[10,32,256]{2,1,0:T(8,128)(2,1)S(1)}, u32[]{:S(2)}, u32[]{:S(2)}) collective-permute-start(bf16[10,32,256]{2,1,0:T(8,128)(2,1)S(1)} %get-tuple-element.38), channel_id=1, source_target_pairs={{0,16},{16,0},{1,17},{17,1},{2,18},{18,2},{3,19},{19,3},{4,20},{20... | collective-permute-start | bytes 491528 | tf_op jit(solution)/shard_map/ppermute | solution.py:855
